TPU v7x, 128 devices: a whole 4x4x4 slice. The times are simulated.
128 devices in a mesh: ckpt: 4 (over z_hi, core), space: 32 (over y, x, z_lo).
Axes of the slice: x: 4, y: 4, z: 4 (z_hi: 2, z_lo: 2; z = z_hi * 2 + z_lo), core: 2. Of those that a mesh axis runs over, the one named last changes fastest.
Arguments:
- checkpoint: float32 [32, 6, 16, 16, 128], P('space', None, 'ckpt'), may hold values from -5 to 5
- seeds: float32 [4, 32, 6, 16, 16, 128], P('ckpt', 'space'), may hold values from -6 to 6
- cell_rate: float32 [32, 16, 16, 128], P('space'), may hold values from 0.5 to 2
- flux_mats: float32 [3, 6, 6], replicated, may hold values from -1.25 to 1.25
- owner: int32 [32], replicated, may hold values from 0 to 31, each once
- neighbours: int32 [32, 6], replicated, may hold values from 0 to 31, as said below
- orientation: int32 [32, 6], replicated, may hold values from 0 to 3, as said below
Outputs:
- adjoint: float32 [4, 32, 6, 16, 16, 128], P('ckpt', 'space')
- final_state: float32 [32, 6, 16, 16, 128], P('space')
Inputs may be any that keep to these rules, and one draw needn't show every extreme that they name: owner lists each space index once. The block across the -x face of neighbours[b, 0] is b, across the +x face of neighbours[b, 1] is b, and likewise for y and z; a block may be its own neighbour. orientation[b, f] equals the code of the same face seen from the block across it.
All inputs are finite; a program needn't handle non-finite values.
Results may differ from a plain program's by a relative error of at most 0.0001.
Values sent between devices are 32-bit elements; how exact they have to be, the bound alone decides.
A program may use at most 128 MiB of HBM per device.

v0:
```python
import jax
import jax.numpy as jnp
from jax import lax
from jax.sharding import PartitionSpec as P

STEPS = 2


time_step = 0.05
damping = 0.015


def boundary(field, side):
    layer_axis = field.ndim - 3 + side // 2
    location = field.shape[layer_axis] - 1 if side % 2 == 0 else 0
    return lax.index_in_dim(field, location, layer_axis, keepdims=False)


def reorient(face, flips):
    face = jnp.where(flips % 2 == 1, jnp.flip(face, -2), face)
    return jnp.where(flips // 2 % 2 == 1, jnp.flip(face, -1), face)


def pad_with(field, ghosts):
    padded = jnp.pad(field, [(0, 0)] + [(1, 1)] * 3)
    for side in range(6):
        layer_axis = side // 2
        location = padded.shape[layer_axis + 1] - 1 if side % 2 == 0 else 0
        if layer_axis == 0:
            padded = padded.at[:, location, 1:-1, 1:-1].set(ghosts[side])
        elif layer_axis == 1:
            padded = padded.at[:, 1:-1, location, 1:-1].set(ghosts[side])
        else:
            padded = padded.at[:, 1:-1, 1:-1, location].set(ghosts[side])
    return padded


def ghost_layer(padded, side):
    layer_axis = side // 2
    location = padded.shape[layer_axis + 1] - 1 if side % 2 == 0 else 0
    if layer_axis == 0:
        return padded[:, location, 1:-1, 1:-1]
    if layer_axis == 1:
        return padded[:, 1:-1, location, 1:-1]
    return padded[:, 1:-1, 1:-1, location]


def add_layer(field, side, layer):
    layer_axis = side // 2
    location = field.shape[layer_axis + 1] - 1 if side % 2 == 0 else 0
    if layer_axis == 0:
        return field.at[:, location].add(layer)
    if layer_axis == 1:
        return field.at[:, :, location].add(layer)
    return field.at[:, :, :, location].add(layer)


def advance(padded, rates, flux_mats):
    interior = padded[:, 1:-1, 1:-1, 1:-1]
    divergence = jnp.zeros_like(interior)
    for direction in range(3):
        if direction == 0:
            strip = padded[:, :, 1:-1, 1:-1]
        elif direction == 1:
            strip = padded[:, 1:-1, :, 1:-1]
        else:
            strip = padded[:, 1:-1, 1:-1, :]
        length = strip.shape[direction + 1]
        left_cells = lax.slice_in_dim(strip, 0, length - 1, axis=direction + 1)
        right_cells = lax.slice_in_dim(strip, 1, length, axis=direction + 1)
        average = 0.5 * (left_cells + right_cells)
        difference = right_cells - left_cells
        spread = jnp.sqrt(1.0 + average[0] * average[0])
        face_flux = (
            jnp.einsum(
                "ij,jxyz->ixyz", flux_mats[direction], average, precision=lax.Precision.HIGHEST
            )
            - 0.5 * spread * difference
        )
        count = face_flux.shape[direction + 1]
        divergence = (
            divergence
            + lax.slice_in_dim(face_flux, 1, count, axis=direction + 1)
            - lax.slice_in_dim(face_flux, 0, count - 1, axis=direction + 1)
        )
    return interior - time_step * rates * divergence - damping * jnp.tanh(interior)


def pick(pieces, sources):
    count = pieces[0].shape[0]
    positions = jnp.arange(count, dtype=jnp.int32)
    result = []
    for side in range(6):
        weight = (positions == sources[side]).astype(jnp.float32)
        piece = pieces[side // 2][:, 1 - side % 2]
        result.append(jnp.sum(weight.reshape((count, 1, 1, 1)) * piece, axis=0))
    return tuple(result)


def side_pairs(layers):
    return [jnp.stack([layers[2 * pair], layers[2 * pair + 1]])[None] for pair in range(3)]


def on_device(checkpoint, seeds, cell_rate, flux_mats, owner, neighbours, orientation):
    restored = lax.all_gather(checkpoint, "ckpt", axis=2, tiled=True)[0]
    rates = cell_rate[0]
    block_count = owner.shape[0]
    indices = jnp.arange(block_count, dtype=jnp.int32)
    position = lax.axis_index("space")
    own_block = jnp.sum(jnp.where(owner == position, indices, 0))
    chosen = (indices == own_block).astype(jnp.int32)[:, None]
    across = jnp.sum(chosen * neighbours, axis=0)
    flips = jnp.sum(chosen * orientation, axis=0)
    sources = jnp.sum(
        (indices[None, :] == across[:, None]).astype(jnp.int32) * owner[None, :], axis=1
    )

    def gather_step(pieces):
        return pick(pieces, sources)

    def fetch(field):
        layers = [boundary(field, side) for side in range(6)]
        x_faces, y_faces, z_faces = side_pairs(layers)
        whole = gather_step(
            (
                lax.all_gather(x_faces, "space", axis=0, tiled=True),
                lax.all_gather(y_faces, "space", axis=0, tiled=True),
                lax.all_gather(z_faces, "space", axis=0, tiled=True),
            )
        )
        return [reorient(whole[side], flips[side]) for side in range(6)]

    padded_states = []
    state = restored
    for section in range(STEPS):
        padded = pad_with(state, fetch(state))
        padded_states.append(padded)
        state = advance(padded, rates, flux_mats)
    adjoint_now = seeds[0, 0]
    for section in reversed(range(STEPS)):
        _, pullback = jax.vjp(lambda grid: advance(grid, rates, flux_mats), padded_states[section])
        cotangent = pullback(adjoint_now)[0]
        x_ghosts, y_ghosts, z_ghosts = side_pairs(
            [ghost_layer(cotangent, side) for side in range(6)]
        )
        incoming = gather_step(
            (
                lax.all_gather(x_ghosts, "space", axis=0, tiled=True),
                lax.all_gather(y_ghosts, "space", axis=0, tiled=True),
                lax.all_gather(z_ghosts, "space", axis=0, tiled=True),
            )
        )
        adjoint_now = cotangent[:, 1:-1, 1:-1, 1:-1]
        for side in range(6):
            adjoint_now = add_layer(adjoint_now, side, reorient(incoming[side], flips[side]))
    return (adjoint_now[None, None], state[None])


def solution(mesh):
    return jax.shard_map(
        on_device,
        mesh=mesh,
        in_specs=(
            P("space", None, "ckpt", None, None),
            P("ckpt", "space", None, None, None, None),
            P("space", None, None, None),
            P(),
            P(),
            P(),
            P(),
        ),
        out_specs=(P("ckpt", "space", None, None, None, None), P("space", None, None, None, None)),
        check_vma=False,
    )
```

profile of v0, /device:TPU:0, one launch (start us, length us, event | category | flops | bytes accessed | tf_op | source)
XLA Modules:
  0.0 1615.2 jit_solution(11246195897142510362)
XLA Ops:
  8.2 11.1 all_gather.39
  42.4 149.0 %all-gather.2 = f32[64,6,16,16]{3,2,1,0:T(8,128)S(1)} all-gather(f32[2,6,16,16]{3,2,1,0:T(8,128)S(1)} %pad_maximum_fusion.2), channel_id=4, replica_groups=mesh['ckpt'=4,'space'=32] {'space'}, dimensions={0}, use_global_device_ids=true | all-gather | bytes 405504 | tf_op jit(solution)/shard_map/all_gather | solution.py:128
  202.7 139.0 %all-gather.21.cloned.1.call-done = f32[64,6,16,128]{3,2,1,0:T(8,128)} async-done(((f32[2,6,16,128]{3,2,1,0:T(8,128)}), f32[64,6,16,128]{3,2,1,0:T(8,128)}) %all-gather.21.cloned.1.call-update) | async-done | bytes 3145744 | tf_op jit(solution)/shard_map/all_gather | solution.py:126
  354.6 19.7 %scatter.44 = f32[6,18,18,130]{3,2,0,1:T(8,128)S(1)} dynamic-update-slice(f32[6,18,18,130]{3,2,0,1:T(8,128)S(1)} %scatter.41, f32[6,16,1,128]{3,2,0,1:T(1,128)} %copy.1412, s32[]{:T(128)} %constant.830.clone.1, s32[]{:T(128)} %constant.831.clone.1, s32[]{:T(128)} %constant.834.clone.1, s32[]{:T(128)} %constant.831.clone.1) | dynamic-update-slice | bytes 98308 | tf_op jit(solution)/shard_map/scatter | solution.py:32
  374.3 19.7 %scatter.45 = f32[6,18,18,130]{3,2,0,1:T(8,128)S(1)} dynamic-update-slice(f32[6,18,18,130]{3,2,0,1:T(8,128)S(1)} %scatter.44, f32[6,16,1,128]{3,2,0,1:T(1,128)} %copy.1414, s32[]{:T(128)} %constant.830.clone.1, s32[]{:T(128)} %constant.831.clone.1, s32[]{:T(128)} %constant.830.clone.1, s32[]{:T(128)} %constant.831.clone.1) | dynamic-update-slice | bytes 98308 | tf_op jit(solution)/shard_map/scatter | solution.py:32
  393.9 23.4 %scatter.46 = f32[6,18,18,130]{3,2,0,1:T(8,128)S(1)} dynamic-update-slice(f32[6,18,18,130]{3,2,0,1:T(8,128)S(1)} %scatter.45, f32[6,16,16,1]{3,2,0,1:T(8,128)} %copy.1417, s32[]{:T(128)} %constant.830.clone.1, s32[]{:T(128)} %constant.831.clone.1, s32[]{:T(128)} %constant.831.clone.1, s32[]{:T(128)} %constant.835.clone.1) | dynamic-update-slice | bytes 12292 | tf_op jit(solution)/shard_map/scatter | solution.py:34
  417.4 12.4 scatter.49
  453.0 148.3 %all-gather.5 = f32[64,6,16,16]{3,2,1,0:T(8,128)S(1)} all-gather(f32[2,6,16,16]{3,2,1,0:T(8,128)S(1)} %pad_maximum_fusion.5), channel_id=7, replica_groups=mesh['ckpt'=4,'space'=32] {'space'}, dimensions={0}, use_global_device_ids=true | all-gather | bytes 405504 | tf_op jit(solution)/shard_map/all_gather | solution.py:128
  619.4 147.3 %all-gather.25.cloned.1.call-done = f32[64,6,16,128]{3,2,1,0:T(8,128)} async-done(((f32[2,6,16,128]{3,2,1,0:T(8,128)}), f32[64,6,16,128]{3,2,1,0:T(8,128)}) %all-gather.25.cloned.1.call-update) | async-done | bytes 3145744 | tf_op jit(solution)/shard_map/all_gather | solution.py:126
  775.2 3.7 scatter.50
  778.9 3.7 scatter.51
  782.6 18.2 %scatter.54 = f32[6,18,18,130]{3,2,0,1:T(8,128)} dynamic-update-slice(f32[6,18,18,130]{3,2,0,1:T(8,128)} %scatter.51, f32[6,16,1,128]{3,2,0,1:T(1,128)} %copy.1436, s32[]{:T(128)} %constant.830.clone.1, s32[]{:T(128)} %constant.831.clone.1, s32[]{:T(128)} %constant.834.clone.1, s32[]{:T(128)} %constant.831.clone.1) | dynamic-update-slice | bytes 98308 | tf_op jit(solution)/shard_map/scatter | solution.py:32
  800.8 18.2 %scatter.55 = f32[6,18,18,130]{3,2,0,1:T(8,128)} dynamic-update-slice(f32[6,18,18,130]{3,2,0,1:T(8,128)} %scatter.54, f32[6,16,1,128]{3,2,0,1:T(1,128)} %copy.1438, s32[]{:T(128)} %constant.830.clone.1, s32[]{:T(128)} %constant.831.clone.1, s32[]{:T(128)} %constant.830.clone.1, s32[]{:T(128)} %constant.831.clone.1) | dynamic-update-slice | bytes 98308 | tf_op jit(solution)/shard_map/scatter | solution.py:32
  819.0 18.2 %scatter.56 = f32[6,18,18,130]{3,2,0,1:T(8,128)} dynamic-update-slice(f32[6,18,18,130]{3,2,0,1:T(8,128)} %scatter.55, f32[6,16,16,1]{3,2,0,1:T(8,128)} %copy.1442, s32[]{:T(128)} %constant.830.clone.1, s32[]{:T(128)} %constant.831.clone.1, s32[]{:T(128)} %constant.831.clone.1, s32[]{:T(128)} %constant.835.clone.1) | dynamic-update-slice | bytes 12292 | tf_op jit(solution)/shard_map/scatter | solution.py:34
  837.1 6.0 scatter.59
  877.8 145.5 %all-gather.8 = f32[64,6,16,16]{3,2,1,0:T(8,128)S(1)} all-gather(f32[2,6,16,16]{3,2,1,0:T(8,128)S(1)} %pad_maximum_fusion.8), channel_id=10, replica_groups=mesh['ckpt'=4,'space'=32] {'space'}, dimensions={0}, use_global_device_ids=true | all-gather | bytes 405504 | tf_op jit(solution)/shard_map/all_gather | solution.py:150
  1040.5 4.0 pad_add_fusion.3
  1060.1 129.3 %all-gather.29.cloned.1.call-done = f32[64,6,16,128]{3,2,1,0:T(8,128)} async-done(((f32[2,6,16,128]{3,2,1,0:T(8,128)}), f32[64,6,16,128]{3,2,1,0:T(8,128)}) %all-gather.29.cloned.1.call-update) | async-done | bytes 3145744 | tf_op jit(solution)/shard_map/all_gather | solution.py:148
  1214.1 9.4 scatter-add.46
  1225.7 3.6 scatter-add.49
  1250.5 145.7 %all-gather.11 = f32[64,6,16,16]{3,2,1,0:T(8,128)S(1)} all-gather(f32[2,6,16,16]{3,2,1,0:T(8,128)S(1)} %pad_maximum_fusion.11), channel_id=13, replica_groups=mesh['ckpt'=4,'space'=32] {'space'}, dimensions={0}, use_global_device_ids=true | all-gather | bytes 405504 | tf_op jit(solution)/shard_map/all_gather | solution.py:150
  1432.3 131.7 %all-gather.33.cloned.1.call-done = f32[64,6,16,128]{3,2,1,0:T(8,128)} async-done(((f32[2,6,16,128]{3,2,1,0:T(8,128)}), f32[64,6,16,128]{3,2,1,0:T(8,128)}) %all-gather.33.cloned.1.call-update) | async-done | bytes 3145744 | tf_op jit(solution)/shard_map/all_gather | solution.py:148
  1587.8 12.2 scatter-add.56
  1601.4 5.8 scatter-add.59
  (378 shorter events, 259.1 us)
Async XLA Ops:
  7.2 15.0 copy-start.54
  7.2 15.0 copy-start.53
  7.2 191.8 %all-gather.23.cloned.1.call-start = ((), (), s32[]{:S(2)}) async-start(), calls=%async_computation.1 | async-start | bytes 3244032 | tf_op jit(solution)/shard_map/all_gather | solution.py:127
  20.1 321.7 %all-gather.21.cloned.1.call-start = ((), (), s32[]{:S(2)}) async-start(), calls=%async_computation | async-start | bytes 3244032 | tf_op jit(solution)/shard_map/all_gather | solution.py:126
  20.8 589.4 %all-gather.27.cloned.1.call-start = ((), (), s32[]{:S(2)}) async-start(), calls=%async_computation.3 | async-start | bytes 3244032 | tf_op jit(solution)/shard_map/all_gather | solution.py:127
  41.7 149.7 %copy-start.41 = (f32[32]{0:T(128)}, f32[32]{0:T(128)S(1)}, u32[]{:S(2)}) copy-start(f32[32]{0:T(128)S(1)} %compare_convert_fusion) | copy-start | bytes 388
  42.4 149.0 %copy-start.45 = (f32[32]{0:T(128)}, f32[32]{0:T(128)S(1)}, u32[]{:S(2)}) copy-start(f32[32]{0:T(128)S(1)} %compare_convert_fusion.1) | copy-start | bytes 388
  196.4 145.3 %copy-start.49 = (f32[32]{0:T(128)}, f32[32]{0:T(128)S(1)}, u32[]{:S(2)}) copy-start(f32[32]{0:T(128)S(1)} %compare_convert_fusion.4) | copy-start | bytes 388
  197.1 144.6 %copy-start.51 = (f32[32]{0:T(128)}, f32[32]{0:T(128)S(1)}, u32[]{:S(2)}) copy-start(f32[32]{0:T(128)S(1)} %compare_convert_fusion.5) | copy-start | bytes 388
  343.9 73.4 %copy-start.15 = (f32[6,16,16,1]{3,2,0,1:T(8,128)S(1)}, f32[6,16,16,1]{3,2,0,1:T(8,128)}, u32[]{:S(2)}) copy-start(f32[6,16,16,1]{3,2,0,1:T(8,128)} %copy.1418) | copy-start | bytes 18436
  442.8 323.9 %all-gather.25.cloned.1.call-start = ((), (), s32[]{:S(2)}) async-start(), calls=%async_computation.2 | async-start | bytes 3244032 | tf_op jit(solution)/shard_map/all_gather | solution.py:126
  444.4 601.4 %all-gather.31.cloned.1.call-start = ((), (), s32[]{:S(2)}) async-start(), calls=%async_computation.5 | async-start | bytes 3244032 | tf_op jit(solution)/shard_map/all_gather | solution.py:149
  453.0 148.3 %copy-start.42 = (f32[32]{0:T(128)S(1)}, f32[32]{0:T(128)}, u32[]{:S(2)}) copy-start(f32[32]{0:T(128)} %copy-done.41) | copy-start | bytes 388
  453.0 148.3 %copy-start.46 = (f32[32]{0:T(128)S(1)}, f32[32]{0:T(128)}, u32[]{:S(2)}) copy-start(f32[32]{0:T(128)} %copy-done.45) | copy-start | bytes 388
  868.6 320.8 %all-gather.29.cloned.1.call-start = ((), (), s32[]{:S(2)}) async-start(), calls=%async_computation.4 | async-start | bytes 3244032 | tf_op jit(solution)/shard_map/all_gather | solution.py:148
  869.4 548.6 %all-gather.35.cloned.1.call-start = ((), (), s32[]{:S(2)}) async-start(), calls=%async_computation.7 | async-start | bytes 3244032 | tf_op jit(solution)/shard_map/all_gather | solution.py:149
  877.8 145.5 %copy-start.43 = (f32[32]{0:T(128)S(1)}, f32[32]{0:T(128)}, u32[]{:S(2)}) copy-start(f32[32]{0:T(128)} %copy-done.41) | copy-start | bytes 388
  877.8 145.5 %copy-start.47 = (f32[32]{0:T(128)S(1)}, f32[32]{0:T(128)}, u32[]{:S(2)}) copy-start(f32[32]{0:T(128)} %copy-done.45) | copy-start | bytes 388
  1246.0 318.0 %all-gather.33.cloned.1.call-start = ((), (), s32[]{:S(2)}) async-start(), calls=%async_computation.6 | async-start | bytes 3244032 | tf_op jit(solution)/shard_map/all_gather | solution.py:148
  1250.5 145.7 %copy-start.44 = (f32[32]{0:T(128)S(1)}, f32[32]{0:T(128)}, u32[]{:S(2)}) copy-start(f32[32]{0:T(128)} %copy-done.41) | copy-start | bytes 388
  1250.5 145.7 %copy-start.48 = (f32[32]{0:T(128)S(1)}, f32[32]{0:T(128)}, u32[]{:S(2)}) copy-start(f32[32]{0:T(128)} %copy-done.45) | copy-start | bytes 388
  1418.0 146.0 %copy-start.50 = (f32[32]{0:T(128)S(1)}, f32[32]{0:T(128)}, u32[]{:S(2)}) copy-start(f32[32]{0:T(128)} %copy-done.49) | copy-start | bytes 388
  1418.0 146.0 %copy-start.52 = (f32[32]{0:T(128)S(1)}, f32[32]{0:T(128)}, u32[]{:S(2)}) copy-start(f32[32]{0:T(128)} %copy-done.51) | copy-start | bytes 388
  1586.0 14.0 copy-start.16
  (40 other events, 100.4 us)
Sparse Core Ops, SparseCore 0:
  20.2 163.9 all-gather.22
  185.8 155.8 all-gather.20
  442.9 165.8 all-gather.26
  610.3 156.4 all-gather.24
  868.7 167.0 all-gather.30
  1037.3 152.0 all-gather.28
  1246.1 164.6 all-gather.34
  1412.5 151.4 all-gather.32
where the time goes:
time: 1630 us; the launch traced here: 1620 us
  blocking collectives  600 us (37%)
  waiting for transfers between devices  547 us (34%)
  local copies, waits for them, and re-layouts  287 us (18%)
  other arithmetic  129 us (8%)
  between operations  31.2 us (2%)
  matrix products  21 us (1%)
    all_gather x2, blocking collectives, fetch(): lax.all_gather(z_faces, 'space', axis=0, tiled=True)  297 us
    all_gather x2, blocking collectives, on_device(): lax.all_gather(z_ghosts, 'space', axis=0, tiled=True)  291 us
    all_gather x2, waiting for transfers between devices, fetch(): lax.all_gather(x_faces, 'space', axis=0, tiled=True)  286 us
    all_gather x2, waiting for transfers between devices, on_device(): lax.all_gather(x_ghosts, 'space', axis=0, tiled=True)  261 us
    scatter x4, local copies, waits for them, and re-layouts, pad_with(): padded = padded.at[:, 1:-1, location, 1:-1].set(ghosts[side])  75.7 us
    scatter x4, local copies, waits for them, and re-layouts, pad_with(): padded = padded.at[:, 1:-1, 1:-1, location].set(ghosts[side])  60 us
  transfers between devices with their start and end apart: 8, of which 4 were waited for; matrix products, arithmetic and copies ran while one was open for 8% of the time, Pallas kernels for 0%

commit v1 on v0

v1 whole, which is shorter than its diff:
```python
import functools

import jax
import jax.numpy as jnp
from jax import lax
from jax.experimental import pallas as pl
from jax.experimental.pallas import tpu as pltpu
from jax.sharding import PartitionSpec as P

MESH = pl.DeviceIdType.MESH
VMEM = pltpu.VMEM
F32 = jnp.float32

NX, NY, NZ, NC = 4, 4, 2, 4
NV, CX, CY, CZ = 6, 16, 16, 128
ROWS = NV * CX * CY
FACE = NV * CX
EXT = (CX + 2) * CY
TAU = 0.05
DAMP = 0.015
HALF = 2 * FACE + CY
QROW = FACE // NC
QA, QB = 2 * QROW + 8, 2 * QROW
SEGS = ((0, FACE), (FACE, FACE), (2 * FACE, CY))
SEGS_QA = ((0, QROW), (QROW, QROW), (2 * QROW, 8))
SEGS_QB = ((0, QROW), (QROW, QROW))


def lanes(shape):
    return lax.broadcasted_iota(jnp.int32, shape, len(shape) - 1)


def rows_of(start, count, step=16):
    return pl.ds(pl.multiple_of(start, step), count)


def pack_xy(src, pa, pb, scale=None):
    for seg, x in ((0, CX - 1), (FACE, 0)):
        for v in range(NV):
            layer = src[pl.ds(v * 256 + x * 16, 16), :]
            if scale is not None:
                layer = layer * (TAU * scale[pl.ds(x * 16, 16), :])
            pa[pl.ds(seg + v * 16, 16), :] = layer
    for seg, y in ((0, CY - 1), (FACE, 0)):
        factor = None
        if scale is not None:
            factor = TAU * scale[pl.ds(y, CX, stride=CY), :]
        for v in range(NV):
            layer = src[pl.ds(v * 256 + y, CX, stride=CY), :]
            if scale is not None:
                layer = layer * factor
            pb[pl.ds(seg + v * 16, 16), :] = layer


def pack_z(values, x, pa, pb):
    lane = lanes((CY, CZ))
    up = pa[pl.ds(2 * FACE, CY), :]
    low = pb[pl.ds(2 * FACE, CY), :]
    for v in range(NV):
        at = v * 16 + x
        here = lane == at
        up = jnp.where(here, pltpu.roll(values[v], at + 1, 1), up)
        low = jnp.where(here, pltpu.roll(values[v], at, 1), low)
    pa[pl.ds(2 * FACE, CY), :] = up
    pb[pl.ds(2 * FACE, CY), :] = low


def clear_z(pa, pb):
    pa[pl.ds(2 * FACE, CY), :] = jnp.zeros((CY, CZ), F32)
    pb[pl.ds(2 * FACE, CY), :] = jnp.zeros((CY, CZ), F32)


def lane_flip(piece, flag):
    lane = lanes(piece.shape)
    return jnp.take_along_axis(piece, lane + flag * (CZ - 1 - 2 * lane), axis=1)


def row_flip(piece, flag):
    row = lax.broadcasted_iota(jnp.int32, (8, CZ), 0)
    index = row + flag * (7 - 2 * row)
    first, second = piece[:8], piece[8:]
    turned = flag == 1
    lower = jnp.where(turned, second, first)
    upper = jnp.where(turned, first, second)
    return jnp.concatenate(
        [jnp.take_along_axis(lower, index, axis=0), jnp.take_along_axis(upper, index, axis=0)]
    )


def place_ghosts(layer, code, ext, gy, gz):
    for f in (0, 1):
        at = (CX + 1) * CY if f == 0 else 0
        for v in range(NV):
            piece = row_flip(layer(f, v), code[f] & 1)
            for h in (0, 8):
                ext[pl.ds(v * EXT + at + h, 8), :] = lane_flip(
                    piece[h : h + 8], (code[f] >> 1) & 1
                )
    for f in (2, 3):
        for v in range(NV):
            piece = layer(f, v)
            for h in (0, 8):
                gy[pl.ds((f - 2) * FACE + v * 16 + h, 8), :] = lane_flip(
                    piece[h : h + 8], (code[f] >> 1) & 1
                )
    for f in (4, 5):
        gz[pl.ds((f - 4) * CY, CY), :] = row_flip(layer(f, 0), (code[f] >> 1) & 1)


def fill_interior(src, ext):
    for v in range(NV):
        ext[pl.ds(v * EXT + CY, CX * CY), :] = src[pl.ds(v * 256, CX * CY), :]


def forward_layers(ghost):
    def face(f):
        start = {1: 0, 0: QROW, 3: QA, 2: QA + QROW}[f]
        return jnp.concatenate([ghost[c, pl.ds(start, QROW), :] for c in range(NC)])

    faces = {f: face(f) for f in range(4)}

    def layer(f, v):
        if f < 4:
            return faces[f][v * 16 : v * 16 + 16]
        c = 0 if f == 5 else 2
        return jnp.concatenate([ghost[c, pl.ds(2 * QROW, 8), :], ghost[c + 1, pl.ds(2 * QROW, 8), :]])

    return layer


def adjoint_layers(ga, gb):
    def layer(f, v):
        half = ga if f in (0, 1, 5) else gb
        if f < 4:
            return half[pl.ds((1 - f % 2) * FACE + v * 16, 16), :]
        return half[pl.ds(2 * FACE, CY), :]

    return layer


def neighbours_of(ext, gy, gz, code, x):
    row = lax.broadcasted_iota(jnp.int32, (CY, CZ), 0)
    lane = lanes((CY, CZ))
    centre = [ext[rows_of(v * EXT + (x + 1) * CY, CY), :] for v in range(NV)]

    def at(direction):
        ups, lows = [], []
        for v in range(NV):
            u = centre[v]
            if direction == 0:
                up = ext[rows_of(v * EXT + (x + 2) * CY, CY), :]
                low = ext[rows_of(v * EXT + x * CY, CY), :]
            elif direction == 1:
                xu = v * 16 + x + (code[2] & 1) * (CX - 1 - 2 * x)
                xl = v * 16 + x + (code[3] & 1) * (CX - 1 - 2 * x)
                up = jnp.where(row == CY - 1, gy[pl.ds(xu, 1), :], pltpu.roll(u, CY - 1, 0))
                low = jnp.where(row == 0, gy[pl.ds(FACE + xl, 1), :], pltpu.roll(u, 1, 0))
            else:
                xu = v * 16 + x + (code[4] & 1) * (CX - 1 - 2 * x)
                xl = v * 16 + x + (code[5] & 1) * (CX - 1 - 2 * x)
                high = pltpu.roll(gz[pl.ds(0, CY), :], CZ - 1 - xu, 1)
                deep = pltpu.roll(gz[pl.ds(CY, CY), :], lax.rem(CZ - xl, CZ), 1)
                up = jnp.where(lane == CZ - 1, high, pltpu.roll(u, CZ - 1, 1))
                low = jnp.where(lane == 0, deep, pltpu.roll(u, 1, 1))
            ups.append(up)
            lows.append(low)
        return ups, lows

    return centre, at


def spread_of(first, second):
    mean = 0.5 * (first + second)
    t = 1.0 + mean * mean
    r = lax.rsqrt(t)
    return t * r, mean * r


def forward_kernel(code, mats, v_ref, ghost, rate, out, pa, pb, ext, gy, gz):
    fill_interior(v_ref, ext)
    place_ghosts(forward_layers(ghost), code, ext, gy, gz)
    clear_z(pa, pb)

    def step(x, carry):
        u, at = neighbours_of(ext, gy, gz, code, x)
        total = [jnp.zeros((CY, CZ), F32) for _ in range(NV)]
        for d in range(3):
            up, low = at(d)
            su, _ = spread_of(up[0], u[0])
            sl, _ = spread_of(u[0], low[0])
            diff = [up[v] - low[v] for v in range(NV)]
            for i in range(NV):
                acc = total[i] - (su * (up[i] - u[i]) - sl * (u[i] - low[i]))
                for j in range(NV):
                    acc = acc + mats[d, i, j] * diff[j]
                total[i] = acc
        tau = (0.5 * TAU) * rate[rows_of(x * CY, CY), :]
        new = [u[v] - tau * total[v] - DAMP * jnp.tanh(u[v]) for v in range(NV)]
        for v in range(NV):
            out[rows_of(v * 256 + x * CY, CY), :] = new[v]
        pack_z(new, x, pa, pb)
        return carry

    lax.fori_loop(0, CX, step, 0)
    pack_xy(out, pa, pb)


def adjoint_body(
    code, mats, ext, gy, gz, wext, wgy, wgz, lam, rate, out, final, pa, pb
):
    def step(x, carry):
        u, at_u = neighbours_of(ext, gy, gz, code, x)
        w, at_w = neighbours_of(wext, wgy, wgz, code, x)
        total = [jnp.zeros((CY, CZ), F32) for _ in range(NV)]
        flux = [jnp.zeros((CY, CZ), F32) for _ in range(NV)]
        tilt = jnp.zeros((CY, CZ), F32)
        for d in range(3):
            up, low = at_u(d)
            wup, wlow = at_w(d)
            su, ru = spread_of(up[0], u[0])
            sl, rl = spread_of(u[0], low[0])
            dot_u = jnp.zeros((CY, CZ), F32)
            dot_l = jnp.zeros((CY, CZ), F32)
            diff = []
            wdiff = []
            for i in range(NV):
                du, dl = up[i] - u[i], u[i] - low[i]
                gu, gl = wup[i] - w[i], w[i] - wlow[i]
                dot_u = dot_u + du * gu
                dot_l = dot_l + dl * gl
                total[i] = total[i] + (su * gu - sl * gl)
                wdiff.append(wup[i] - wlow[i])
                if final is not None:
                    flux[i] = flux[i] - (su * du - sl * dl)
                    diff.append(up[i] - low[i])
            tilt = tilt + ru * dot_u + rl * dot_l
            for i in range(NV):
                acc = total[i]
                for j in range(NV):
                    acc = acc + mats[d, j, i] * wdiff[j]
                total[i] = acc
            if final is not None:
                for i in range(NV):
                    acc = flux[i]
                    for j in range(NV):
                        acc = acc + mats[d, i, j] * diff[j]
                    flux[i] = acc
        tau = TAU * rate[rows_of(x * CY, CY), :]
        packed = []
        for v in range(NV):
            here = rows_of(v * 256 + x * CY, CY)
            bent = jnp.tanh(u[v])
            old = lam[here, :]
            new = old - DAMP * (1.0 - bent * bent) * old + 0.5 * total[v]
            if v == 0:
                new = new - 0.25 * tilt
            out[here, :] = new
            if final is not None:
                final[here, :] = u[v] - (0.5 * tau) * flux[v] - DAMP * bent
            packed.append(tau * new)
        if pa is not None:
            pack_z(packed, x, pa, pb)
        return carry

    lax.fori_loop(0, CX, step, 0)


def fill_weighted(lam, rate, wext):
    for v in range(NV):
        wext[pl.ds(v * EXT + CY, CX * CY), :] = lam[pl.ds(v * 256, CX * CY), :] * (TAU * rate[...])


def adjoint_mid_kernel(
    code, mats, v_ref, ghost, rate, lam, wa, wb, final, out, pa, pb, ext, gy, gz, wext, wgy, wgz
):
    fill_interior(v_ref, ext)
    place_ghosts(forward_layers(ghost), code, ext, gy, gz)
    fill_weighted(lam, rate, wext)
    place_ghosts(adjoint_layers(wa, wb), code, wext, wgy, wgz)
    clear_z(pa, pb)
    adjoint_body(code, mats, ext, gy, gz, wext, wgy, wgz, lam, rate, out, final, pa, pb)
    pack_xy(out, pa, pb, rate)


def adjoint_end_kernel(
    code, mats, v_ref, ghost, rate, lam, wa, wb, out, ext, gy, gz, wext, wgy, wgz
):
    fill_interior(v_ref, ext)
    place_ghosts(forward_layers(ghost), code, ext, gy, gz)
    fill_weighted(lam, rate, wext)
    place_ghosts(adjoint_layers(wa, wb), code, wext, wgy, wgz)
    adjoint_body(code, mats, ext, gy, gz, wext, wgy, wgz, lam, rate, out, None, None, None)


class Place:
    def __init__(self):
        self.c = lax.axis_index("ckpt")
        s = lax.axis_index("space")
        self.z = lax.rem(s, NZ)
        self.x = lax.rem(lax.div(s, NZ), NX)
        self.y = lax.div(s, NZ * NX)

    def space(self, x, y, z):
        return (y * NX + x) * NZ + z

    def along_x(self, k):
        return (self.c, self.space(lax.rem(self.x + k, NX), self.y, self.z))

    def along_y(self, k):
        return (self.c, self.space(self.x, lax.rem(self.y + k, NY), self.z))

    def across_z(self):
        return (self.c, self.space(self.x, self.y, 1 - self.z))

    def member(self, k):
        return (lax.rem(self.c + k, NC), lax.axis_index("space"))


def greet(place, members):
    barrier = pltpu.get_barrier_semaphore()
    partners = [place.across_z()]
    partners += [place.along_x(k) for k in range(1, NX)]
    partners += [place.along_y(k) for k in range(1, NY)]
    if members:
        partners += [place.member(k) for k in range(1, NC)]
    for partner in partners:
        pl.semaphore_signal(barrier, inc=1, device_id=partner, device_id_type=MESH)
    return lambda: pl.semaphore_wait(barrier, len(partners))


class Tables:
    def __init__(self, place, owner, links):
        self.place = place
        spots = [place.space(place.x, lax.rem(place.y + k, NY), place.z) for k in range(NY)]
        spots += [place.space(lax.rem(place.x + k, NX), place.y, place.z) for k in range(1, NX)]

        def find(b, found):
            who = owner[b]
            return tuple(jnp.where(who == s, b, f) for f, s in zip(found, spots))

        blocks = lax.fori_loop(0, NX * NY * NZ, find, tuple(jnp.int32(0) for _ in spots))
        self.own = blocks[0]
        self.down = {"A": list(blocks[:NY]), "B": [blocks[0]] + list(blocks[NY:])}
        self.owner, self.links = owner, links

    def source(self, block, layer):
        s = self.owner[self.links[block, layer ^ 1]]
        return lax.rem(lax.div(s, NZ), NX), lax.div(s, NZ * NX), lax.rem(s, NZ)

    def slot(self, half, k, layer):
        x, y, z = self.source(self.down[half][k], layer)
        turn = jnp.where(z == self.place.z, 0, 1)
        if half == "A":
            return turn * NX + lax.rem(self.place.x - x + NX, NX)
        return turn * NY + lax.rem(self.place.y - y + NY, NY)

    def last(self, half, layer):
        x, y, _ = self.source(self.own, layer)
        if half == "A":
            return lax.rem(self.place.y - y + NY, NY)
        return lax.rem(self.place.x - x + NX, NX)


RING = NX
HOPS = (2, 1, 3)
N_COPIES = 2 + 6 * len(HOPS)


class Exchange:
    def __init__(self, place, bufs, outs, arrivals, send, recv, base):
        self.place, self.bufs, self.outs, self.arrivals = place, bufs, outs, arrivals
        self.send, self.recv, self.base = send, recv, base
        self.all = []
        self.first = {"A": place.along_x, "B": place.along_y}
        self.second = {"A": place.along_y, "B": place.along_x}
        self.across, self.own, self.passed, self.final = {}, {}, {}, {}

    def copy(self, src, dst, device):
        n = self.base + len(self.all)
        made = pltpu.make_async_remote_copy(
            src_ref=src,
            dst_ref=dst,
            send_sem=self.send.at[n],
            recv_sem=self.recv.at[n],
            device_id=device,
            device_id_type=MESH,
        )
        made.start()
        self.all.append(made)
        return made

    def begin(self):
        for half in "AB":
            buf = self.bufs[half]
            self.across[half] = self.copy(buf.at[0], buf.at[RING], self.place.across_z())
        self.own = {"A": [], "B": []}
        for k in HOPS:
            for half in "AB":
                buf = self.bufs[half]
                self.own[half].append(self.copy(buf.at[0], buf.at[k], self.first[half](k)))

    def relay(self):
        self.passed = {"A": [], "B": []}
        for half in "AB":
            self.across[half].wait_recv()
        for k in HOPS:
            for half in "AB":
                buf = self.bufs[half]
                self.passed[half].append(self.copy(buf.at[RING], buf.at[RING + k], self.first[half](k)))

    def hand_on(self, tables, segments):
        self.final = {"A": [], "B": []}
        for half in "AB":
            for made in self.own[half] + self.passed[half]:
                made.wait_recv()
            buf, out, arrive = self.bufs[half], self.outs[half], self.arrivals[half]
            for k in HOPS + (0,):
                for start, count, layer in segments[half]:
                    picked = buf[tables.slot(half, k, layer), pl.ds(start, count), :]
                    if k == 0:
                        arrive[0, pl.ds(start, count), :] = picked
                    else:
                        out[k - 1, pl.ds(start, count), :] = picked
                if k:
                    self.final[half].append(
                        self.copy(out.at[k - 1], arrive.at[k], self.second[half](k))
                    )

    def take(self, tables, segments, put):
        for half in "AB":
            for made in self.final[half]:
                made.wait_recv()
            for start, count, layer in segments[half]:
                put(half, start, count, self.arrivals[half][tables.last(half, layer), pl.ds(start, count), :])

    def drain(self):
        for made in self.all:
            made.wait_send()


def full_segments():
    return {
        "A": [(s, n, f) for (s, n), f in zip(SEGS, (0, 1, 4))],
        "B": [(s, n, f) for (s, n), f in zip(SEGS, (2, 3, 5))],
    }


def quarter_segments(c):
    zface = jnp.where(c < 2, 4, 5)
    return {
        "A": [(s, n, f) for (s, n), f in zip(SEGS_QA, (0, 1, zface))],
        "B": [(s, n, f) for (s, n), f in zip(SEGS_QB, (2, 3))],
    }


def exchange_scratch(ra, rb):
    return [
        VMEM((2 * RING, ra, CZ), F32),
        VMEM((2 * RING, rb, CZ), F32),
        VMEM((RING - 1, ra, CZ), F32),
        VMEM((RING - 1, rb, CZ), F32),
        VMEM((RING, ra, CZ), F32),
        VMEM((RING, rb, CZ), F32),
    ]


def exchange_of(place, scratch, send, recv, base):
    ba, bb, oa, ob, ra, rb = scratch
    return Exchange(place, {"A": ba, "B": bb}, {"A": oa, "B": ob}, {"A": ra, "B": rb}, send, recv, base)


def quarter_packet(c, pa, pb, ba, bb):
    part = rows_of(c * QROW, QROW, 8)
    part2 = rows_of(FACE + c * QROW, QROW, 8)
    ba[0, pl.ds(0, QROW), :] = pa[part, :]
    ba[0, pl.ds(QROW, QROW), :] = pa[part2, :]
    bb[0, pl.ds(0, QROW), :] = pb[part, :]
    bb[0, pl.ds(QROW, QROW), :] = pb[part2, :]
    zrows = rows_of(2 * FACE + lax.rem(c, 2) * 8, 8, 8)
    ba[0, pl.ds(2 * QROW, 8), :] = jnp.where(c < 2, pa[zrows, :], pb[zrows, :])


def share(place, mine, ghost, send, recv, base):
    made = []
    for k in range(1, NC):
        copy = pltpu.make_async_remote_copy(
            src_ref=mine,
            dst_ref=ghost.at[place.c],
            send_sem=send.at[base + k - 1],
            recv_sem=recv.at[base + k - 1],
            device_id=place.member(k),
            device_id_type=MESH,
        )
        copy.start()
        made.append(copy)
    ghost[place.c] = mine[...]
    return made


def open_kernel(
    owner, links, codes, part, seeds, rate, state, ghost, wa, wb, code, *scratch
):
    fwd, adj = scratch[0:6], scratch[6:12]
    pa, pb, mine, stored, landed, send, recv = scratch[12:]
    place = Place()
    met = greet(place, True)
    pack_xy(seeds, pa, pb, rate)
    clear_z(pa, pb)

    def seed_z(x, carry):
        tau = TAU * rate[rows_of(x * CY, CY), :]
        pack_z([seeds[rows_of(v * 256 + x * CY, CY), :] * tau for v in range(NV)], x, pa, pb)
        return carry

    lax.fori_loop(0, CX, seed_z, 0)
    adj[0][0] = pa[...]
    adj[1][0] = pb[...]
    met()
    parts = []
    for k in range(1, NC):
        copy = pltpu.make_async_remote_copy(
            src_ref=part,
            dst_ref=stored.at[place.c],
            send_sem=send.at[k - 1],
            recv_sem=recv.at[k - 1],
            device_id=place.member(k),
            device_id_type=MESH,
        )
        copy.start()
        parts.append(copy)
    stored[place.c] = part[...]
    late = exchange_of(place, adj, send, recv, 6 + N_COPIES)
    late.begin()
    tables = Tables(place, owner, links)
    for f in range(6):
        code[f] = codes[tables.own, f]
    for copy in parts:
        copy.wait_recv()
    span = CX * CY // NC
    for c in range(NC):
        for v in range(NV):
            state[pl.ds(v * 256 + c * span, span), :] = stored[c, pl.ds(v * span, span), :]
    pack_xy(state, pa, pb)
    clear_z(pa, pb)

    def state_z(x, carry):
        pack_z([state[rows_of(v * 256 + x * CY, CY), :] for v in range(NV)], x, pa, pb)
        return carry

    lax.fori_loop(0, CX, state_z, 0)
    quarter_packet(place.c, pa, pb, fwd[0], fwd[1])
    early = exchange_of(place, fwd, send, recv, 6)
    early.begin()
    early.relay()
    late.relay()
    quarters = quarter_segments(place.c)
    early.hand_on(tables, quarters)

    def put_mine(half, start, count, value):
        mine[pl.ds((0 if half == "A" else QA) + start, count), :] = value

    early.take(tables, quarters, put_mine)
    shared = share(place, mine, landed, send, recv, 3)
    wholes = full_segments()
    late.hand_on(tables, wholes)

    def put_whole(half, start, count, value):
        (wa if half == "A" else wb)[pl.ds(start, count), :] = value

    late.take(tables, wholes, put_whole)
    for copy in shared:
        copy.wait_recv()
    ghost[...] = landed[...]
    for copy in parts + shared:
        copy.wait_send()
    early.drain()
    late.drain()


def forward_exchange_kernel(owner, links, pa, pb, ghost, *scratch):
    fwd = scratch[0:6]
    mine, landed, send, recv = scratch[6:]
    place = Place()
    met = greet(place, True)
    quarter_packet(place.c, pa, pb, fwd[0], fwd[1])
    met()
    early = exchange_of(place, fwd, send, recv, 3)
    early.begin()
    tables = Tables(place, owner, links)
    early.relay()
    quarters = quarter_segments(place.c)
    early.hand_on(tables, quarters)

    def put_mine(half, start, count, value):
        mine[pl.ds((0 if half == "A" else QA) + start, count), :] = value

    early.take(tables, quarters, put_mine)
    shared = share(place, mine, landed, send, recv, 0)
    for copy in shared:
        copy.wait_recv()
    ghost[...] = landed[...]
    for copy in shared:
        copy.wait_send()
    early.drain()


def adjoint_exchange_kernel(owner, links, pa, pb, wa, wb, *scratch):
    adj = scratch[0:6]
    send, recv = scratch[6:]
    place = Place()
    met = greet(place, False)
    adj[0][0] = pa[...]
    adj[1][0] = pb[...]
    met()
    late = exchange_of(place, adj, send, recv, 0)
    late.begin()
    tables = Tables(place, owner, links)
    late.relay()
    wholes = full_segments()
    late.hand_on(tables, wholes)

    def put_whole(half, start, count, value):
        (wa if half == "A" else wb)[pl.ds(start, count), :] = value

    late.take(tables, wholes, put_whole)
    late.drain()


def spec(space):
    return pl.BlockSpec(memory_space=space)


def shape(*dims):
    return jax.ShapeDtypeStruct(dims, F32)


def call(kernel, ins, outs, scratch, ident=None):
    return pl.pallas_call(
        kernel,
        out_shape=tuple(s for _, s in outs),
        in_specs=[spec(m) for m in ins],
        out_specs=tuple(spec(m) for m, _ in outs),
        scratch_shapes=scratch,
        compiler_params=pltpu.CompilerParams(
            collective_id=ident, has_side_effects=ident is not None
        ),
    )


def on_device(checkpoint, seeds, cell_rate, flux_mats, owner, neighbours, orientation):
    vm, sm = pltpu.VMEM, pltpu.SMEM
    part = checkpoint.reshape(ROWS // NC, CZ)
    rate = cell_rate.reshape(CX * CY, CZ)
    lam = seeds.reshape(ROWS, CZ)
    sems = lambda n: [pltpu.SemaphoreType.DMA((n,)), pltpu.SemaphoreType.DMA((n,))]
    quarter, whole = exchange_scratch(QA, QB), exchange_scratch(HALF, HALF)
    half = shape(HALF, CZ)
    ghosts = shape(NC, QA + QB, CZ)
    block = shape(ROWS, CZ)

    state, ghost0, wa, wb, code = call(
        open_kernel,
        (sm, sm, sm, vm, vm, vm),
        (
            (vm, block),
            (vm, ghosts),
            (vm, half),
            (vm, half),
            (sm, jax.ShapeDtypeStruct((8,), jnp.int32)),
        ),
        quarter
        + whole
        + [VMEM((HALF, CZ), F32), VMEM((HALF, CZ), F32), VMEM((QA + QB, CZ), F32)]
        + [VMEM((NC, ROWS // NC, CZ), F32), VMEM((NC, QA + QB, CZ), F32)]
        + sems(6 + 2 * N_COPIES),
        0,
    )(owner, neighbours, orientation, part, lam, rate)

    stencil = [VMEM((NV * EXT, CZ), F32), VMEM((2 * FACE, CZ), F32), VMEM((2 * CY, CZ), F32)]
    state1, pa, pb = call(
        forward_kernel, (sm, sm, vm, vm, vm), ((vm, block), (vm, half), (vm, half)), stencil
    )(code, flux_mats, state, ghost0, rate)

    (ghost1,) = call(
        forward_exchange_kernel,
        (sm, sm, vm, vm),
        ((vm, ghosts),),
        quarter + [VMEM((QA + QB, CZ), F32), VMEM((NC, QA + QB, CZ), F32)] + sems(3 + N_COPIES),
        1,
    )(owner, neighbours, pa, pb)

    final, lam1, pa, pb = call(
        adjoint_mid_kernel,
        (sm, sm) + (vm,) * 6,
        ((vm, block), (vm, block), (vm, half), (vm, half)),
        stencil * 2,
    )(code, flux_mats, state1, ghost1, rate, lam, wa, wb)

    wa, wb = call(
        adjoint_exchange_kernel,
        (sm, sm, vm, vm),
        ((vm, half), (vm, half)),
        whole + sems(N_COPIES),
        2,
    )(owner, neighbours, pa, pb)

    (lam0,) = call(
        adjoint_end_kernel, (sm, sm) + (vm,) * 6, ((vm, block),), stencil * 2
    )(code, flux_mats, state, ghost0, rate, lam1, wa, wb)
    return (
        lam0.reshape(1, 1, NV, CX, CY, CZ),
        final.reshape(1, NV, CX, CY, CZ),
    )


def solution(mesh):
    return jax.shard_map(
        on_device,
        mesh=mesh,
        in_specs=(
            P("space", None, "ckpt", None, None),
            P("ckpt", "space", None, None, None, None),
            P("space", None, None, None),
            P(),
            P(),
            P(),
            P(),
        ),
        out_specs=(P("ckpt", "space", None, None, None, None), P("space", None, None, None, None)),
        check_vma=False,
    )
```

time: 1630 us -> 110 us (0.07)
  blocking collectives: 600 us -> 0 us
  waiting for transfers between devices: 547 us -> 0 us
  local copies, waits for them, and re-layouts: 287 us -> 2.06 us
  other arithmetic: 129 us -> 0 us
  Pallas kernels: 0 us -> 106 us
  between operations: 31.2 us -> 0.67 us
  matrix products: 21 us -> 0 us
    all_gather x5 -> x0, blocking collectives: 600 us -> none  [the longest x2 297 us: fetch(): lax.all_gather(z_faces, 'space', axis=0, tiled=True)]
    all_gather x8 -> x0, waiting for transfers between devices: 547 us -> none  [the longest x2 286 us: fetch(): lax.all_gather(x_faces, 'space', axis=0, tiled=True)]
    scatter x12 -> x0, local copies, waits for them, and re-layouts: 149 us -> none  [the longest x4 75.7 us: pad_with(): padded = padded.at[:, 1:-1, location, 1:-1].set(ghosts[side])]
    pallas_call x0 -> x6, Pallas kernels: none -> 106 us  [the longest x1 42.3 us: on_device(): call(open_kernel, (sm, sm, sm, vm, vm, vm), ((vm, block), (vm, ghosts), (...]
    rev x48 -> x0, local copies, waits for them, and re-layouts: 45.8 us -> none  [the longest x24 23.8 us: reorient(): return jnp.where(flips // 2 % 2 == 1, jnp.flip(face, -1), face)]
    scatter-add x8 -> x0, local copies, waits for them, and re-layouts: 41.9 us -> none  [the longest x4 31 us: add_layer(): return field.at[:, :, :, location].add(layer)]
    reduce_sum x19 -> x0, other arithmetic: 27.2 us -> none  [the longest x12 22.7 us: pick(): result.append(jnp.sum(weight.reshape((count, 1, 1, 1)) * piece, axis=0))]
    another operation x34 -> x0, other arithmetic: 22.6 us -> none
  transfers between devices with their start and end apart: 8 -> 0, of which waited for: 4 -> 0; matrix products, arithmetic and copies ran while one was open for 8% -> 0% of each run, Pallas kernels for 0% -> 0%
where the time goes in v1:
time: 110 us; the launch traced here: 109 us
  Pallas kernels  106 us (96%)
  local copies, waits for them, and re-layouts  2.06 us (2%)
    pallas_call x1, Pallas kernels, on_device(): call(open_kernel, (sm, sm, sm, vm, vm, vm), ((vm, block), (vm, ghosts), (...  42.3 us
    pallas_call x1, Pallas kernels, on_device(): call(adjoint_exchange_kernel, (sm, sm, vm, vm), ((vm, half), (vm, half)),...  23 us
    pallas_call x1, Pallas kernels, on_device(): call(forward_exchange_kernel, (sm, sm, vm, vm), ((vm, ghosts),), quarter...  18.9 us
    pallas_call x1, Pallas kernels, on_device(): call(adjoint_mid_kernel, (sm, sm) + (vm,) * 6, ((vm, block), (vm, block),...  9.3 us
    pallas_call x1, Pallas kernels, on_device(): call(adjoint_end_kernel, (sm, sm) + (vm,) * 6, ((vm, block),), stencil * 2)  7.01 us
    pallas_call x1, Pallas kernels, on_device(): call(forward_kernel, (sm, sm, vm, vm, vm), ((vm, block), (vm, half), (vm,...  6.04 us

profile of v1, /device:TPU:0, one launch (start us, length us, event | category | flops | bytes accessed | tf_op | source)
XLA Modules:
  0.0 109.2 jit_solution(515845844383211366)
XLA Ops:
  0.6 0.0 copy-start
  0.6 0.7 copy-done
  1.3 0.0 copy-start.1
  1.3 0.7 copy.9.links
  2.0 0.0 copy-done.1
  2.0 0.7 copy.10.codes
  2.7 42.3 %shard_map.86 = (f32[1536,128]{1,0:T(8,128)}, f32[4,104,128]{2,1,0:T(8,128)}, f32[208,128]{1,0:T(8,128)}, f32[208,128]{1,0:T(8,128)}, s32[8]{0:T(128)}) custom-call(s32[32]{0:T(128)} %owner.5, s32[32,6]{1,0:T(8,128)} %copy.9.links, s32[32,6]{1,0:T(8,128)} %copy.10.codes, f32[384,128]{1,0:T(8,128)} %bitcast.12, f32[1536,128]{1,0:T(8,128)} %bitcast.5, ...), custom_call_target="tpu_custom_call" | custom-call | tf_op jit(solution)/shard_map/pallas_call | solution.py:661
  45.0 6.0 %shard_map.87 = (f32[1536,128]{1,0:T(8,128)}, f32[208,128]{1,0:T(8,128)}, f32[208,128]{1,0:T(8,128)}) custom-call(s32[8]{0:T(128)} %get-tuple-element.16.code, f32[3,6,6]{2,1,0:T(8,128)} %mats.5, f32[1536,128]{1,0:T(8,128)} %get-tuple-element.17.v_ref, f32[4,104,128]{2,1,0:T(8,128)} %get-tuple-element.18.ghost, f32[256,128]{1,0:T(8,128)} %bitcast.8), custom_call_target="tpu_custom_call" | custom-call | tf_op jit(solution)/shard_map/pallas_call | solution.py:680
  51.0 18.9 %shard_map.88.ghost = f32[4,104,128]{2,1,0:T(8,128)} custom-call(s32[32]{0:T(128)} %owner.5, s32[32,6]{1,0:T(8,128)} %copy.9.links, f32[208,128]{1,0:T(8,128)} %get-tuple-element.20.pa, f32[208,128]{1,0:T(8,128)} %get-tuple-element.21.pb), custom_call_target="tpu_custom_call" | custom-call | tf_op jit(solution)/shard_map/pallas_call | solution.py:684
  69.9 9.3 %shard_map.89 = (f32[1536,128]{1,0:T(8,128)}, f32[1536,128]{1,0:T(8,128)}, f32[208,128]{1,0:T(8,128)}, f32[208,128]{1,0:T(8,128)}) custom-call(s32[8]{0:T(128)} %get-tuple-element.16.code, f32[3,6,6]{2,1,0:T(8,128)} %mats.5, f32[1536,128]{1,0:T(8,128)} %get-tuple-element.19.v_ref, f32[4,104,128]{2,1,0:T(8,128)} %shard_map.88.ghost, f32[256,128]{1,0:T(8,128)} %bitcast.9, ...), custom_call_target="tpu_custom_call" | custom-call | tf_op jit(solution)/shard_map/pallas_call | solution.py:692
  79.2 23.0 %shard_map.90 = (f32[208,128]{1,0:T(8,128)}, f32[208,128]{1,0:T(8,128)}) custom-call(s32[32]{0:T(128)} %owner.5, s32[32,6]{1,0:T(8,128)} %copy.9.links, f32[208,128]{1,0:T(8,128)} %get-tuple-element.25.pa, f32[208,128]{1,0:T(8,128)} %get-tuple-element.26.pb), custom_call_target="tpu_custom_call" | custom-call | tf_op jit(solution)/shard_map/pallas_call | solution.py:699
  102.1 7.0 %shard_map.91 = f32[1536,128]{1,0:T(8,128)} custom-call(s32[8]{0:T(128)} %get-tuple-element.16.code, f32[3,6,6]{2,1,0:T(8,128)} %mats.5, f32[1536,128]{1,0:T(8,128)} %get-tuple-element.17.v_ref, f32[4,104,128]{2,1,0:T(8,128)} %get-tuple-element.18.ghost, f32[256,128]{1,0:T(8,128)} %bitcast.10, f32[1536,128]{1,0:T(8,128)} %get-tuple-element.24.lam, ...), custom_call_target="tpu_custom_call" | custom-call | tf_op jit(solution)/shard_map/pallas_call | solution.py:707
Async XLA Ops:
  0.6 0.7 copy-start
  1.3 0.7 copy-start.1

commit v2 on v1

v2 whole, which is shorter than its diff:
```python
import jax
import jax.numpy as jnp
from jax import lax
from jax.experimental import pallas as pl
from jax.experimental.pallas import tpu as pltpu
from jax.sharding import PartitionSpec as P

MESH = pl.DeviceIdType.MESH
VMEM = pltpu.VMEM
F32 = jnp.float32

NX, NY, NZ, NC = 4, 4, 2, 4
NV, CX, CY, CZ = 6, 16, 16, 128
ROWS = NV * CX * CY
FACE = NV * CX
EXT = (CX + 2) * CY
TAU = 0.05
DAMP = 0.015
HALF = 2 * FACE + CY
QROW = FACE // NC
QA, QB = 2 * QROW + 8, 2 * QROW
SEGS = ((0, FACE), (FACE, FACE), (2 * FACE, CY))
SEGS_QA = ((0, QROW), (QROW, QROW), (2 * QROW, 8))
SEGS_QB = ((0, QROW), (QROW, QROW))


def lanes(shape):
    return lax.broadcasted_iota(jnp.int32, shape, len(shape) - 1)


def rows_of(start, count, step=16):
    return pl.ds(pl.multiple_of(start, step), count)


def cell_rows(v, x):
    return rows_of(v * EXT + (x + 1) * CY, CY)


def pack_xy(ext, pa, pb):
    for seg, x in ((0, CX - 1), (FACE, 0)):
        for v in range(NV):
            pa[pl.ds(seg + v * 16, 16), :] = ext[pl.ds(v * EXT + (x + 1) * CY, CY), :]
    for seg, y in ((0, CY - 1), (FACE, 0)):
        for v in range(NV):
            pb[pl.ds(seg + v * 16, 16), :] = ext[pl.ds(v * EXT + CY + y, CX, stride=CY), :]


def pack_z(values, x, pa, pb):
    lane = lanes((CY, CZ))
    up = pa[pl.ds(2 * FACE, CY), :]
    low = pb[pl.ds(2 * FACE, CY), :]
    for v in range(NV):
        at = v * 16 + x
        here = lane == at
        up = jnp.where(here, pltpu.roll(values[v], at + 1, 1), up)
        low = jnp.where(here, pltpu.roll(values[v], at, 1), low)
    pa[pl.ds(2 * FACE, CY), :] = up
    pb[pl.ds(2 * FACE, CY), :] = low


def clear_z(pa, pb):
    pa[pl.ds(2 * FACE, CY), :] = jnp.zeros((CY, CZ), F32)
    pb[pl.ds(2 * FACE, CY), :] = jnp.zeros((CY, CZ), F32)


def lane_flip(piece, flag, width):
    lane = lanes(piece.shape)
    at = lane & (width - 1)
    return jnp.take_along_axis(piece, lane + flag * (width - 1 - 2 * at), axis=1)


def row_flip(piece, flag):
    row = lax.broadcasted_iota(jnp.int32, (8, CZ), 0)
    index = row + flag * (7 - 2 * row)
    first, second = piece[:8], piece[8:]
    turned = flag == 1
    lower = jnp.where(turned, second, first)
    upper = jnp.where(turned, first, second)
    return [jnp.take_along_axis(lower, index, axis=0), jnp.take_along_axis(upper, index, axis=0)]


def place_ghosts(layer, code, ext, gy, gz):
    for f in range(6):
        first, second = code[f] & 1, (code[f] >> 1) & 1
        if f < 4:
            for v in range(NV):
                for h, piece in enumerate(row_flip(layer(f, v), first)):
                    piece = lane_flip(piece, second, CZ)
                    if f < 2:
                        start = v * EXT + ((CX + 1) * CY if f == 0 else 0)
                        ext[pl.ds(start + 8 * h, 8), :] = piece
                    else:
                        gy[pl.ds((f - 2) * FACE + v * 16 + 8 * h, 8), :] = piece
        else:
            for h, piece in enumerate(row_flip(layer(f, 0), second)):
                gz[pl.ds((f - 4) * CY + 8 * h, 8), :] = lane_flip(piece, first, CX)


def forward_layers(ghost):
    def face(f):
        start = {1: 0, 0: QROW, 3: QA, 2: QA + QROW}[f]
        return jnp.concatenate([ghost[c, pl.ds(start, QROW), :] for c in range(NC)])

    faces = {f: face(f) for f in range(4)}

    def layer(f, v):
        if f < 4:
            return faces[f][v * 16 : v * 16 + 16]
        c = 0 if f == 5 else 2
        return jnp.concatenate([ghost[c, pl.ds(2 * QROW, 8), :], ghost[c + 1, pl.ds(2 * QROW, 8), :]])

    return layer


def adjoint_layers(ga, gb):
    def layer(f, v):
        half = ga if f in (0, 1, 5) else gb
        if f < 4:
            return half[pl.ds((1 - f % 2) * FACE + v * 16, 16), :]
        return half[pl.ds(2 * FACE, CY), :]

    return layer


def neighbours_of(grid, x):
    ext, gy, gz = grid
    row = lax.broadcasted_iota(jnp.int32, (CY, CZ), 0)
    lane = lanes((CY, CZ))
    centre = [ext[cell_rows(v, x), :] for v in range(NV)]

    def at(direction):
        ups, lows = [], []
        for v in range(NV):
            u = centre[v]
            at_x = v * 16 + x
            if direction == 0:
                up = ext[cell_rows(v, x + 1), :]
                low = ext[cell_rows(v, x - 1), :]
            elif direction == 1:
                up = jnp.where(row == CY - 1, gy[pl.ds(at_x, 1), :], pltpu.roll(u, CY - 1, 0))
                low = jnp.where(row == 0, gy[pl.ds(FACE + at_x, 1), :], pltpu.roll(u, 1, 0))
            else:
                high = pltpu.roll(gz[pl.ds(0, CY), :], CZ - 1 - at_x, 1)
                deep = pltpu.roll(gz[pl.ds(CY, CY), :], lax.rem(CZ - at_x, CZ), 1)
                up = jnp.where(lane == CZ - 1, high, pltpu.roll(u, CZ - 1, 1))
                low = jnp.where(lane == 0, deep, pltpu.roll(u, 1, 1))
            ups.append(up)
            lows.append(low)
        return ups, lows

    return centre, at


def spread_of(first, second):
    mean = 0.5 * (first + second)
    t = 1.0 + mean * mean
    r = lax.rsqrt(t)
    return t * r, mean * r


def forward_step(mats, rate, grid, out, pa, pb, x):
    u, at = neighbours_of(grid, x)
    total = [jnp.zeros((CY, CZ), F32) for _ in range(NV)]
    for d in range(3):
        up, low = at(d)
        su, _ = spread_of(up[0], u[0])
        sl, _ = spread_of(u[0], low[0])
        diff = [up[v] - low[v] for v in range(NV)]
        for i in range(NV):
            acc = total[i] - (su * (up[i] - u[i]) - sl * (u[i] - low[i]))
            for j in range(NV):
                acc = acc + mats[d, i, j] * diff[j]
            total[i] = acc
    tau = (0.5 * TAU) * rate[rows_of(x * CY, CY), :]
    new = [u[v] - tau * total[v] - DAMP * jnp.tanh(u[v]) for v in range(NV)]
    for v in range(NV):
        out[cell_rows(v, x), :] = new[v]
    pack_z(new, x, pa, pb)


def adjoint_step(mats, rate, grid, wgrid, lam, out, x, final=None, weighted=None, pa=None, pb=None):
    u, at_u = neighbours_of(grid, x)
    w, at_w = neighbours_of(wgrid, x)
    total = [jnp.zeros((CY, CZ), F32) for _ in range(NV)]
    flux = [jnp.zeros((CY, CZ), F32) for _ in range(NV)]
    tilt = jnp.zeros((CY, CZ), F32)
    for d in range(3):
        up, low = at_u(d)
        wup, wlow = at_w(d)
        su, ru = spread_of(up[0], u[0])
        sl, rl = spread_of(u[0], low[0])
        dot_u = jnp.zeros((CY, CZ), F32)
        dot_l = jnp.zeros((CY, CZ), F32)
        diff = []
        wdiff = []
        for i in range(NV):
            du, dl = up[i] - u[i], u[i] - low[i]
            gu, gl = wup[i] - w[i], w[i] - wlow[i]
            dot_u = dot_u + du * gu
            dot_l = dot_l + dl * gl
            total[i] = total[i] + (su * gu - sl * gl)
            wdiff.append(wup[i] - wlow[i])
            if final is not None:
                flux[i] = flux[i] - (su * du - sl * dl)
                diff.append(up[i] - low[i])
        tilt = tilt + ru * dot_u + rl * dot_l
        for i in range(NV):
            acc = total[i]
            for j in range(NV):
                acc = acc + mats[d, j, i] * wdiff[j]
            total[i] = acc
        if final is not None:
            for i in range(NV):
                acc = flux[i]
                for j in range(NV):
                    acc = acc + mats[d, i, j] * diff[j]
                flux[i] = acc
    tau = TAU * rate[rows_of(x * CY, CY), :]
    packed = []
    for v in range(NV):
        here = rows_of(v * 256 + x * CY, CY)
        bent = jnp.tanh(u[v])
        old = lam[here, :]
        new = old - DAMP * (1.0 - bent * bent) * old + 0.5 * total[v]
        if v == 0:
            new = new - 0.25 * tilt
        out[here, :] = new
        if final is not None:
            final[here, :] = u[v] - (0.5 * tau) * flux[v] - DAMP * bent
            packed.append(tau * new)
            weighted[cell_rows(v, x), :] = packed[v]
    if final is not None:
        pack_z(packed, x, pa, pb)


def each_x(step, start=0, stop=CX):
    def body(x, carry):
        step(x)
        return carry

    lax.fori_loop(start, stop, body, 0)


class Place:
    def __init__(self):
        self.c = lax.axis_index("ckpt")
        s = lax.axis_index("space")
        self.z = lax.rem(s, NZ)
        self.x = lax.rem(lax.div(s, NZ), NX)
        self.y = lax.div(s, NZ * NX)

    def space(self, x, y, z):
        return (y * NX + x) * NZ + z

    def along_x(self, k):
        return (self.c, self.space(lax.rem(self.x + k, NX), self.y, self.z))

    def along_y(self, k):
        return (self.c, self.space(self.x, lax.rem(self.y + k, NY), self.z))

    def across_z(self):
        return (self.c, self.space(self.x, self.y, 1 - self.z))

    def member(self, k):
        return (lax.rem(self.c + k, NC), lax.axis_index("space"))


def greet(place, members):
    barrier = pltpu.get_barrier_semaphore()
    partners = [place.across_z()]
    partners += [place.along_x(k) for k in range(1, NX)]
    partners += [place.along_y(k) for k in range(1, NY)]
    if members:
        partners += [place.member(k) for k in range(1, NC)]
    for partner in partners:
        pl.semaphore_signal(barrier, inc=1, device_id=partner, device_id_type=MESH)
    return lambda: pl.semaphore_wait(barrier, len(partners))


class Tables:
    def __init__(self, place, owner, links):
        self.place = place
        spots = [place.space(place.x, lax.rem(place.y + k, NY), place.z) for k in range(NY)]
        spots += [place.space(lax.rem(place.x + k, NX), place.y, place.z) for k in range(1, NX)]

        def find(b, found):
            who = owner[b]
            return tuple(jnp.where(who == s, b, f) for f, s in zip(found, spots))

        blocks = lax.fori_loop(0, NX * NY * NZ, find, tuple(jnp.int32(0) for _ in spots))
        self.own = blocks[0]
        self.down = {"A": list(blocks[:NY]), "B": [blocks[0]] + list(blocks[NY:])}
        self.owner, self.links = owner, links

    def source(self, block, layer):
        s = self.owner[self.links[block, layer ^ 1]]
        return lax.rem(lax.div(s, NZ), NX), lax.div(s, NZ * NX), lax.rem(s, NZ)

    def slot(self, half, k, layer):
        x, y, z = self.source(self.down[half][k], layer)
        turn = jnp.where(z == self.place.z, 0, 1)
        if half == "A":
            return turn * NX + lax.rem(self.place.x - x + NX, NX)
        return turn * NY + lax.rem(self.place.y - y + NY, NY)

    def last(self, half, layer):
        x, y, _ = self.source(self.own, layer)
        if half == "A":
            return lax.rem(self.place.y - y + NY, NY)
        return lax.rem(self.place.x - x + NX, NX)


RING = NX
HOPS = (2, 1, 3)
N_COPIES = 2 + 6 * len(HOPS)


class Exchange:
    def __init__(self, place, bufs, outs, arrivals, send, recv, base):
        self.place, self.bufs, self.outs, self.arrivals = place, bufs, outs, arrivals
        self.send, self.recv, self.base = send, recv, base
        self.all = []
        self.first = {"A": place.along_x, "B": place.along_y}
        self.second = {"A": place.along_y, "B": place.along_x}
        self.across, self.own, self.passed, self.final = {}, {}, {}, {}

    def copy(self, src, dst, device):
        n = self.base + len(self.all)
        made = pltpu.make_async_remote_copy(
            src_ref=src,
            dst_ref=dst,
            send_sem=self.send.at[n],
            recv_sem=self.recv.at[n],
            device_id=device,
            device_id_type=MESH,
        )
        made.start()
        self.all.append(made)
        return made

    def begin(self):
        for half in "AB":
            buf = self.bufs[half]
            self.across[half] = self.copy(buf.at[0], buf.at[RING], self.place.across_z())
        self.own = {"A": [], "B": []}
        for k in HOPS:
            for half in "AB":
                buf = self.bufs[half]
                self.own[half].append(self.copy(buf.at[0], buf.at[k], self.first[half](k)))

    def relay(self):
        self.passed = {"A": [], "B": []}
        for half in "AB":
            self.across[half].wait_recv()
        for k in HOPS:
            for half in "AB":
                buf = self.bufs[half]
                self.passed[half].append(self.copy(buf.at[RING], buf.at[RING + k], self.first[half](k)))

    def hand_on(self, tables, segments):
        self.final = {"A": [], "B": []}
        for half in "AB":
            for made in self.own[half] + self.passed[half]:
                made.wait_recv()
            buf, out, arrive = self.bufs[half], self.outs[half], self.arrivals[half]
            for k in HOPS + (0,):
                for start, count, layer in segments[half]:
                    picked = buf[tables.slot(half, k, layer), pl.ds(start, count), :]
                    if k == 0:
                        arrive[0, pl.ds(start, count), :] = picked
                    else:
                        out[k - 1, pl.ds(start, count), :] = picked
                if k:
                    self.final[half].append(
                        self.copy(out.at[k - 1], arrive.at[k], self.second[half](k))
                    )

    def take(self, tables, segments, put):
        for half in "AB":
            for made in self.final[half]:
                made.wait_recv()
            for start, count, layer in segments[half]:
                put(half, start, count, self.arrivals[half][tables.last(half, layer), pl.ds(start, count), :])

    def drain(self):
        for made in self.all:
            made.wait_send()


def full_segments():
    return {
        "A": [(s, n, f) for (s, n), f in zip(SEGS, (0, 1, 4))],
        "B": [(s, n, f) for (s, n), f in zip(SEGS, (2, 3, 5))],
    }


def quarter_segments(c):
    zface = jnp.where(c < 2, 4, 5)
    return {
        "A": [(s, n, f) for (s, n), f in zip(SEGS_QA, (0, 1, zface))],
        "B": [(s, n, f) for (s, n), f in zip(SEGS_QB, (2, 3))],
    }


def exchange_scratch(ra, rb):
    return [
        VMEM((2 * RING, ra, CZ), F32),
        VMEM((2 * RING, rb, CZ), F32),
        VMEM((RING - 1, ra, CZ), F32),
        VMEM((RING - 1, rb, CZ), F32),
        VMEM((RING, ra, CZ), F32),
        VMEM((RING, rb, CZ), F32),
    ]


def exchange_of(place, scratch, send, recv, base):
    ba, bb, oa, ob, ra, rb = scratch
    return Exchange(place, {"A": ba, "B": bb}, {"A": oa, "B": ob}, {"A": ra, "B": rb}, send, recv, base)


def quarter_packet(c, pa, pb, ba, bb):
    part = rows_of(c * QROW, QROW, 8)
    part2 = rows_of(FACE + c * QROW, QROW, 8)
    ba[0, pl.ds(0, QROW), :] = pa[part, :]
    ba[0, pl.ds(QROW, QROW), :] = pa[part2, :]
    bb[0, pl.ds(0, QROW), :] = pb[part, :]
    bb[0, pl.ds(QROW, QROW), :] = pb[part2, :]
    zrows = rows_of(2 * FACE + lax.rem(c, 2) * 8, 8, 8)
    ba[0, pl.ds(2 * QROW, 8), :] = jnp.where(c < 2, pa[zrows, :], pb[zrows, :])


def share(place, mine, ghost, send, recv, base):
    made = []
    for k in range(1, NC):
        copy = pltpu.make_async_remote_copy(
            src_ref=mine,
            dst_ref=ghost.at[place.c],
            send_sem=send.at[base + k - 1],
            recv_sem=recv.at[base + k - 1],
            device_id=place.member(k),
            device_id_type=MESH,
        )
        copy.start()
        made.append(copy)
    ghost[place.c] = mine[...]
    return made


def put_into(mine):
    def put(half, start, count, value):
        mine[pl.ds((0 if half == "A" else QA) + start, count), :] = value

    return put


def put_halves(wa, wb):
    def put(half, start, count, value):
        (wa if half == "A" else wb)[pl.ds(start, count), :] = value

    return put


def kernel(owner, links, codes, mats, part, seeds, rate, adjoint, final, *scratch):
    first, second = scratch[0:6], scratch[6:12]
    third, fourth = scratch[12:18], scratch[18:24]
    grid0, grid1, wgrid, wgrid1 = (scratch[24 + 3 * n : 27 + 3 * n] for n in range(4))
    pa, pb, mine, mine1, stored, landed, landed1, wa, wb, lam, send, recv = scratch[36:]
    place = Place()
    met = greet(place, True)

    clear_z(pa, pb)

    def weigh(x):
        tau = TAU * rate[rows_of(x * CY, CY), :]
        values = [seeds[rows_of(v * 256 + x * CY, CY), :] * tau for v in range(NV)]
        for v in range(NV):
            wgrid[0][cell_rows(v, x), :] = values[v]
        pack_z(values, x, pa, pb)

    each_x(weigh)
    pack_xy(wgrid[0], pa, pb)
    third[0][0] = pa[...]
    third[1][0] = pb[...]
    met()

    parts = []
    for k in range(1, NC):
        copy = pltpu.make_async_remote_copy(
            src_ref=part,
            dst_ref=stored.at[place.c],
            send_sem=send.at[k - 1],
            recv_sem=recv.at[k - 1],
            device_id=place.member(k),
            device_id_type=MESH,
        )
        copy.start()
        parts.append(copy)
    stored[place.c] = part[...]
    tables = Tables(place, owner, links)
    code = [codes[tables.own, f] for f in range(6)]
    for copy in parts:
        copy.wait_recv()
    span = CX * CY // NC
    for c in range(NC):
        for v in range(NV):
            grid0[0][pl.ds(v * EXT + CY + c * span, span), :] = stored[c, pl.ds(v * span, span), :]
    pack_xy(grid0[0], pa, pb)
    clear_z(pa, pb)
    each_x(lambda x: pack_z([grid0[0][cell_rows(v, x), :] for v in range(NV)], x, pa, pb))

    quarters, wholes = quarter_segments(place.c), full_segments()
    early = exchange_of(place, first, send, recv, 9)
    late = exchange_of(place, third, send, recv, 9 + N_COPIES)
    again = exchange_of(place, second, send, recv, 9 + 2 * N_COPIES)
    back = exchange_of(place, fourth, send, recv, 9 + 3 * N_COPIES)

    quarter_packet(place.c, pa, pb, first[0], first[1])
    early.begin()
    early.relay()
    early.hand_on(tables, quarters)
    early.take(tables, quarters, put_into(mine))
    shared = share(place, mine, landed, send, recv, 3)
    late.begin()
    clear_z(pa, pb)
    for copy in shared:
        copy.wait_recv()
    place_ghosts(forward_layers(landed), code, *grid0)

    def forward(x):
        forward_step(mats, rate, grid0, grid1[0], pa, pb, x)

    each_x(forward, 0, CX // 2)
    late.relay()
    each_x(forward, CX // 2, CX)
    pack_xy(grid1[0], pa, pb)

    quarter_packet(place.c, pa, pb, second[0], second[1])
    again.begin()
    again.relay()
    late.hand_on(tables, wholes)
    again.hand_on(tables, quarters)
    again.take(tables, quarters, put_into(mine1))
    shared1 = share(place, mine1, landed1, send, recv, 6)
    late.take(tables, wholes, put_halves(wa, wb))
    place_ghosts(adjoint_layers(wa, wb), code, *wgrid)
    clear_z(pa, pb)
    for copy in shared1:
        copy.wait_recv()
    place_ghosts(forward_layers(landed1), code, *grid1)

    def middle(x):
        adjoint_step(mats, rate, grid1, wgrid, seeds, lam, x, final, wgrid1[0], pa, pb)

    each_x(middle)
    pack_xy(wgrid1[0], pa, pb)

    fourth[0][0] = pa[...]
    fourth[1][0] = pb[...]
    back.begin()
    back.relay()
    back.hand_on(tables, wholes)
    back.take(tables, wholes, put_halves(wa, wb))
    place_ghosts(adjoint_layers(wa, wb), code, *wgrid1)
    each_x(lambda x: adjoint_step(mats, rate, grid0, wgrid1, lam, adjoint, x))

    for copy in parts + shared + shared1:
        copy.wait_send()
    for exchange in (early, late, again, back):
        exchange.drain()


def on_device(checkpoint, seeds, cell_rate, flux_mats, owner, neighbours, orientation):
    vm, sm = pltpu.VMEM, pltpu.SMEM
    block = jax.ShapeDtypeStruct((ROWS, CZ), F32)
    quarter, whole = exchange_scratch(QA, QB), exchange_scratch(HALF, HALF)
    grid = [VMEM((NV * EXT, CZ), F32), VMEM((2 * FACE, CZ), F32), VMEM((2 * CY, CZ), F32)]
    half = VMEM((HALF, CZ), F32)
    mine, landed = VMEM((QA + QB, CZ), F32), VMEM((NC, QA + QB, CZ), F32)
    copies = 9 + 4 * N_COPIES
    adjoint, final = pl.pallas_call(
        kernel,
        out_shape=(block, block),
        in_specs=[pl.BlockSpec(memory_space=m) for m in (sm, sm, sm, sm, vm, vm, vm)],
        out_specs=(pl.BlockSpec(memory_space=vm), pl.BlockSpec(memory_space=vm)),
        scratch_shapes=quarter * 2
        + whole * 2
        + grid * 4
        + [half, half, mine, mine, VMEM((NC, ROWS // NC, CZ), F32), landed, landed, half, half]
        + [VMEM((ROWS, CZ), F32)]
        + [pltpu.SemaphoreType.DMA((copies,)), pltpu.SemaphoreType.DMA((copies,))],
        compiler_params=pltpu.CompilerParams(collective_id=0, has_side_effects=True),
    )(
        owner,
        neighbours,
        orientation,
        flux_mats,
        checkpoint.reshape(ROWS // NC, CZ),
        seeds.reshape(ROWS, CZ),
        cell_rate.reshape(CX * CY, CZ),
    )
    return (
        adjoint.reshape(1, 1, NV, CX, CY, CZ),
        final.reshape(1, NV, CX, CY, CZ),
    )


def solution(mesh):
    return jax.shard_map(
        on_device,
        mesh=mesh,
        in_specs=(
            P("space", None, "ckpt", None, None),
            P("ckpt", "space", None, None, None, None),
            P("space", None, None, None),
            P(),
            P(),
            P(),
            P(),
        ),
        out_specs=(P("ckpt", "space", None, None, None, None), P("space", None, None, None, None)),
        check_vma=False,
    )
```

time: 110 us -> 98 us (0.89)
  Pallas kernels: 106 us -> 91.1 us
  local copies, waits for them, and re-layouts: 2.06 us -> 5.12 us
    pallas_call x6 -> x1, Pallas kernels: 106 us -> 91.1 us  [on_device(): pl.pallas_call(kernel, out_shape=(block, block), in_specs=[pl.BlockSpec(m...]
    unnamed x6 -> x10, local copies, waits for them, and re-layouts: 2.06 us -> 5.12 us
where the time goes in v2:
time: 98 us; the launch traced here: 96.9 us
  Pallas kernels  91.1 us (93%)
  local copies, waits for them, and re-layouts  5.12 us (5%)
    pallas_call x1, Pallas kernels, on_device(): pl.pallas_call(kernel, out_shape=(block, block), in_specs=[pl.BlockSpec(m...  91.1 us
    unnamed x10, local copies, waits for them, and re-layouts  5.12 us

profile of v2, /device:TPU:0, one launch (start us, length us, event | category | flops | bytes accessed | tf_op | source)
XLA Modules:
  0.0 96.9 jit_solution(7104083748074367906)
XLA Ops:
  0.6 0.0 copy-start.1
  0.6 0.7 copy-done.1
  1.3 0.0 copy-start.2
  1.3 0.7 copy.9.links
  2.0 0.0 copy-done.2
  2.0 0.7 copy.10.codes
  2.7 91.1 %shard_map.86 = (f32[1536,128]{1,0:T(8,128)}, f32[1536,128]{1,0:T(8,128)}) custom-call(s32[32]{0:T(128)} %owner.1, s32[32,6]{1,0:T(8,128)} %copy.9.links, s32[32,6]{1,0:T(8,128)} %copy.10.codes, f32[3,6,6]{2,1,0:T(8,128)} %mats.1, f32[384,128]{1,0:T(8,128)} %bitcast.8, f32[1536,128]{1,0:T(8,128)} %bitcast.7, f32[256,128]{1,0:T(8,128)} %bitcast.9), custom_call_target="tpu_custom_call" | custom-call | tf_op jit(solution)/shard_map/pallas_call | solution.py:580
  93.8 0.0 copy-start
  93.9 2.2 %copy.13 = f32[1,1,6,16,16,128]{5,4,3,2,1,0:T(8,128)} copy(f32[1,1,6,16,16,128]{5,4,3,2,1,0:T(8,128)} %bitcast.6) | data formatting | bytes 1572864
  96.0 0.0 copy-done
  96.0 0.9 copy.14
Async XLA Ops:
  0.6 0.7 copy-start.1
  1.3 0.7 copy-start.2
  93.8 2.2 %copy-start = (f32[1536,128]{1,0:T(8,128)S(1)}, f32[1536,128]{1,0:T(8,128)}, u32[]{:S(2)}) copy-start(f32[1536,128]{1,0:T(8,128)} %get-tuple-element.5) | copy-start | bytes 2359300

commit v3 on v2

--- a/solution.py
+++ b/solution.py
@@ -22,6 +22,9 @@
 SEGS = ((0, FACE), (FACE, FACE), (2 * FACE, CY))
 SEGS_QA = ((0, QROW), (QROW, QROW), (2 * QROW, 8))
 SEGS_QB = ((0, QROW), (QROW, QROW))
+STRIP = CX // NC
+QX = 2 * QROW + CY
+SEGS_QX = ((0, QROW), (QROW, QROW), (2 * QROW, CY))
 
 
 def lanes(shape):
@@ -110,6 +113,135 @@
         return jnp.concatenate([ghost[c, pl.ds(2 * QROW, 8), :], ghost[c + 1, pl.ds(2 * QROW, 8), :]])
 
     return layer
+
+
+def strip_layers(ghost):
+    lane = lanes((CY, CZ))
+
+    def layer(f, v):
+        if f < 2:
+            start = (1 - f) * QROW
+            rows = range(v * 16, v * 16 + 16, 8)
+            return jnp.concatenate(
+                [ghost[r // QROW, pl.ds(start + r % QROW, 8), :] for r in rows]
+            )
+        if f < 4:
+            start = QX + (3 - f) * QROW + v * STRIP
+            return jnp.concatenate([ghost[c, pl.ds(start, STRIP), :] for c in range(NC)])
+        start = 2 * QROW if f == 5 else QX + 2 * QROW
+        out = ghost[0, pl.ds(start, CY), :]
+        for c in range(1, NC):
+            out = jnp.where((lane & 15) // STRIP == c, ghost[c, pl.ds(start, CY), :], out)
+        return out
+
+    return layer
+
+
+def pack_strip(part, c, xface, ba, bb):
+    lane = lanes((CY, CZ))
+    for seg, y in ((0, CY - 1), (QROW, 0)):
+        for v in range(NV):
+            bb[0, pl.ds(seg + v * STRIP, STRIP), :] = part[pl.ds(v * 64 + y, STRIP, stride=CY), :]
+    up = jnp.zeros((CY, CZ), F32)
+    low = jnp.zeros((CY, CZ), F32)
+    for v in range(NV):
+        for x in range(STRIP):
+            value = part[pl.ds(v * 64 + x * CY, CY), :]
+            at = v * 16 + c * STRIP + x
+            here = lane == at
+            up = jnp.where(here, pltpu.roll(value, at + 1, 1), up)
+            low = jnp.where(here, pltpu.roll(value, at, 1), low)
+            if x == STRIP - 1:
+                xface[0, pl.ds(v * 16, 16), :] = value
+            if x == 0:
+                xface[1, pl.ds(v * 16, 16), :] = value
+    ba[0, pl.ds(2 * QROW, CY), :] = up
+    bb[0, pl.ds(2 * QROW, CY), :] = low
+
+
+class EndLayers:
+    def __init__(self, place, xface, share, send, recv, base):
+        self.place, self.xface, self.share = place, xface, share
+        self.send, self.recv, self.base = send, recv, base
+
+    def copy(self, n, who, member):
+        return pltpu.make_async_remote_copy(
+            src_ref=self.xface.at[n, pl.ds(member * QROW, QROW)],
+            dst_ref=self.share.at[n],
+            send_sem=self.send.at[self.base + n * NC + member],
+            recv_sem=self.recv.at[self.base + n],
+            device_id=(member, lax.axis_index("space")),
+            device_id_type=MESH,
+        )
+
+    def each(self, holder, other):
+        for n, who in ((0, NC - 1), (1, 0)):
+            members = [m for m in range(NC) if m != who]
+            if holder is not None:
+
+                @pl.when(self.place.c == who)
+                def _():
+                    holder(n, who, members)
+
+            if other is not None:
+
+                @pl.when(self.place.c != who)
+                def _():
+                    other(n, who, members)
+
+    def begin(self):
+        def give(n, who, members):
+            for m in members:
+                self.copy(n, who, m).start()
+            self.share[n] = self.xface[n, pl.ds(who * QROW, QROW), :]
+
+        self.each(give, None)
+
+    def take(self):
+        self.each(None, lambda n, who, members: self.copy(n, who, members[0]).wait_recv())
+
+    def drain(self):
+        self.each(lambda n, who, members: [self.copy(n, who, m).wait_send() for m in members], None)
+
+
+class Gather:
+    def __init__(self, place, part, stored, send, recv, base):
+        self.place, self.part, self.stored = place, part, stored
+        self.send, self.recv, self.base = send, recv, base
+        self.all = []
+
+    def copy(self, src, slot, member):
+        n = self.base + len(self.all)
+        made = pltpu.make_async_remote_copy(
+            src_ref=src,
+            dst_ref=self.stored.at[slot],
+            send_sem=self.send.at[n],
+            recv_sem=self.recv.at[n],
+            device_id=(member, lax.axis_index("space")),
+            device_id_type=MESH,
+        )
+        made.start()
+        self.all.append(made)
+
+    def begin(self):
+        c = self.place.c
+        self.core = c + 1 - 2 * lax.rem(c, 2)
+        self.far = lax.rem(c + 2, NC)
+        self.copy(self.part, c, self.far)
+        self.copy(self.part, c, self.core)
+        self.stored[c] = self.part[...]
+
+    def relay(self):
+        self.all[0].wait_recv()
+        self.copy(self.stored.at[self.far], self.far, self.core)
+
+    def take(self):
+        for made in self.all[1:]:
+            made.wait_recv()
+
+    def drain(self):
+        for made in self.all:
+            made.wait_send()
 
 
 def adjoint_layers(ga, gb):
@@ -293,7 +425,7 @@
         self.owner, self.links = owner, links
 
     def source(self, block, layer):
-        s = self.owner[self.links[block, layer ^ 1]]
+        s = self.owner[self.links[layer ^ 1, block]]
         return lax.rem(lax.div(s, NZ), NX), lax.div(s, NZ * NX), lax.rem(s, NZ)
 
     def slot(self, half, k, layer):
@@ -338,13 +470,16 @@
         self.all.append(made)
         return made
 
-    def begin(self):
-        for half in "AB":
+    def send_across(self, halves="AB"):
+        for half in halves:
             buf = self.bufs[half]
             self.across[half] = self.copy(buf.at[0], buf.at[RING], self.place.across_z())
-        self.own = {"A": [], "B": []}
+
+    def send_own(self, halves="AB"):
+        for half in halves:
+            self.own[half] = []
         for k in HOPS:
-            for half in "AB":
+            for half in halves:
                 buf = self.bufs[half]
                 self.own[half].append(self.copy(buf.at[0], buf.at[k], self.first[half](k)))
 
@@ -402,6 +537,13 @@
     }
 
 
+def strip_segments():
+    return {
+        "A": [(s, n, f) for (s, n), f in zip(SEGS_QX, (0, 1, 4))],
+        "B": [(s, n, f) for (s, n), f in zip(SEGS_QX, (2, 3, 5))],
+    }
+
+
 def exchange_scratch(ra, rb):
     return [
         VMEM((2 * RING, ra, CZ), F32),
@@ -446,9 +588,9 @@
     return made
 
 
-def put_into(mine):
+def put_into(mine, second):
     def put(half, start, count, value):
-        mine[pl.ds((0 if half == "A" else QA) + start, count), :] = value
+        mine[pl.ds((0 if half == "A" else second) + start, count), :] = value
 
     return put
 
@@ -464,9 +606,29 @@
     first, second = scratch[0:6], scratch[6:12]
     third, fourth = scratch[12:18], scratch[18:24]
     grid0, grid1, wgrid, wgrid1 = (scratch[24 + 3 * n : 27 + 3 * n] for n in range(4))
-    pa, pb, mine, mine1, stored, landed, landed1, wa, wb, lam, send, recv = scratch[36:]
+    pa, pb, mine, mine1, stored, landed, landed1, wa, wb, lam, xface, xshare, send, recv = scratch[36:]
     place = Place()
+    early = exchange_of(place, first, send, recv, 0)
+    late = exchange_of(place, third, send, recv, N_COPIES)
+    again = exchange_of(place, second, send, recv, 2 * N_COPIES)
+    back = exchange_of(place, fourth, send, recv, 3 * N_COPIES)
+    base = 4 * N_COPIES
+    gather = Gather(place, part, stored, send, recv, base + 6)
+    ends = EndLayers(place, xface, xshare, send, recv, base + 9)
+    strips, quarters, wholes = strip_segments(), quarter_segments(place.c), full_segments()
+
     met = greet(place, True)
+    pack_strip(part, place.c, xface, first[0], first[1])
+    met()
+    ends.begin()
+    early.send_across("B")
+    early.send_own("B")
+    ends.take()
+    for n in range(2):
+        first[0][0, pl.ds(n * QROW, QROW), :] = xshare[n]
+    early.send_across("A")
+    early.send_own("A")
+    gather.begin()
 
     clear_z(pa, pb)
 
@@ -481,66 +643,37 @@
     pack_xy(wgrid[0], pa, pb)
     third[0][0] = pa[...]
     third[1][0] = pb[...]
-    met()
-
-    parts = []
-    for k in range(1, NC):
-        copy = pltpu.make_async_remote_copy(
-            src_ref=part,
-            dst_ref=stored.at[place.c],
-            send_sem=send.at[k - 1],
-            recv_sem=recv.at[k - 1],
-            device_id=place.member(k),
-            device_id_type=MESH,
-        )
-        copy.start()
-        parts.append(copy)
-    stored[place.c] = part[...]
+    early.relay()
+    late.send_across()
     tables = Tables(place, owner, links)
-    code = [codes[tables.own, f] for f in range(6)]
-    for copy in parts:
-        copy.wait_recv()
+    code = [codes[f, tables.own] for f in range(6)]
+    gather.relay()
+    early.hand_on(tables, strips)
+    late.send_own()
+    early.take(tables, strips, put_into(mine, QX))
+    shared = share(place, mine, landed, send, recv, base)
+    gather.take()
     span = CX * CY // NC
     for c in range(NC):
         for v in range(NV):
             grid0[0][pl.ds(v * EXT + CY + c * span, span), :] = stored[c, pl.ds(v * span, span), :]
-    pack_xy(grid0[0], pa, pb)
     clear_z(pa, pb)
-    each_x(lambda x: pack_z([grid0[0][cell_rows(v, x), :] for v in range(NV)], x, pa, pb))
-
-    quarters, wholes = quarter_segments(place.c), full_segments()
-    early = exchange_of(place, first, send, recv, 9)
-    late = exchange_of(place, third, send, recv, 9 + N_COPIES)
-    again = exchange_of(place, second, send, recv, 9 + 2 * N_COPIES)
-    back = exchange_of(place, fourth, send, recv, 9 + 3 * N_COPIES)
-
-    quarter_packet(place.c, pa, pb, first[0], first[1])
-    early.begin()
-    early.relay()
-    early.hand_on(tables, quarters)
-    early.take(tables, quarters, put_into(mine))
-    shared = share(place, mine, landed, send, recv, 3)
-    late.begin()
-    clear_z(pa, pb)
+    late.relay()
     for copy in shared:
         copy.wait_recv()
-    place_ghosts(forward_layers(landed), code, *grid0)
-
-    def forward(x):
-        forward_step(mats, rate, grid0, grid1[0], pa, pb, x)
-
-    each_x(forward, 0, CX // 2)
-    late.relay()
-    each_x(forward, CX // 2, CX)
+    place_ghosts(strip_layers(landed), code, *grid0)
+
+    each_x(lambda x: forward_step(mats, rate, grid0, grid1[0], pa, pb, x))
     pack_xy(grid1[0], pa, pb)
 
     quarter_packet(place.c, pa, pb, second[0], second[1])
-    again.begin()
+    again.send_across()
+    again.send_own()
     again.relay()
     late.hand_on(tables, wholes)
     again.hand_on(tables, quarters)
-    again.take(tables, quarters, put_into(mine1))
-    shared1 = share(place, mine1, landed1, send, recv, 6)
+    again.take(tables, quarters, put_into(mine1, QA))
+    shared1 = share(place, mine1, landed1, send, recv, base + 3)
     late.take(tables, wholes, put_halves(wa, wb))
     place_ghosts(adjoint_layers(wa, wb), code, *wgrid)
     clear_z(pa, pb)
@@ -556,43 +689,48 @@
 
     fourth[0][0] = pa[...]
     fourth[1][0] = pb[...]
-    back.begin()
+    back.send_across()
+    back.send_own()
     back.relay()
     back.hand_on(tables, wholes)
     back.take(tables, wholes, put_halves(wa, wb))
     place_ghosts(adjoint_layers(wa, wb), code, *wgrid1)
     each_x(lambda x: adjoint_step(mats, rate, grid0, wgrid1, lam, adjoint, x))
 
-    for copy in parts + shared + shared1:
+    for copy in shared + shared1:
         copy.wait_send()
-    for exchange in (early, late, again, back):
+    ends.drain()
+    for exchange in (gather, early, late, again, back):
         exchange.drain()
 
 
 def on_device(checkpoint, seeds, cell_rate, flux_mats, owner, neighbours, orientation):
     vm, sm = pltpu.VMEM, pltpu.SMEM
     block = jax.ShapeDtypeStruct((ROWS, CZ), F32)
-    quarter, whole = exchange_scratch(QA, QB), exchange_scratch(HALF, HALF)
+    strip, quarter = exchange_scratch(QX, QX), exchange_scratch(QA, QB)
+    whole = exchange_scratch(HALF, HALF)
     grid = [VMEM((NV * EXT, CZ), F32), VMEM((2 * FACE, CZ), F32), VMEM((2 * CY, CZ), F32)]
     half = VMEM((HALF, CZ), F32)
-    mine, landed = VMEM((QA + QB, CZ), F32), VMEM((NC, QA + QB, CZ), F32)
-    copies = 9 + 4 * N_COPIES
+    copies = 17 + 4 * N_COPIES
     adjoint, final = pl.pallas_call(
         kernel,
         out_shape=(block, block),
         in_specs=[pl.BlockSpec(memory_space=m) for m in (sm, sm, sm, sm, vm, vm, vm)],
         out_specs=(pl.BlockSpec(memory_space=vm), pl.BlockSpec(memory_space=vm)),
-        scratch_shapes=quarter * 2
+        scratch_shapes=strip
+        + quarter
         + whole * 2
         + grid * 4
-        + [half, half, mine, mine, VMEM((NC, ROWS // NC, CZ), F32), landed, landed, half, half]
-        + [VMEM((ROWS, CZ), F32)]
+        + [half, half, VMEM((2 * QX, CZ), F32), VMEM((QA + QB, CZ), F32)]
+        + [VMEM((NC, ROWS // NC, CZ), F32)]
+        + [VMEM((NC, 2 * QX, CZ), F32), VMEM((NC, QA + QB, CZ), F32), half, half]
+        + [VMEM((ROWS, CZ), F32), VMEM((2, FACE, CZ), F32), VMEM((2, QROW, CZ), F32)]
         + [pltpu.SemaphoreType.DMA((copies,)), pltpu.SemaphoreType.DMA((copies,))],
         compiler_params=pltpu.CompilerParams(collective_id=0, has_side_effects=True),
     )(
         owner,
-        neighbours,
-        orientation,
+        neighbours.T,
+        orientation.T,
         flux_mats,
         checkpoint.reshape(ROWS // NC, CZ),
         seeds.reshape(ROWS, CZ),

time: 98 us -> 88.6 us (0.904)
  Pallas kernels: 91.1 us -> 83.9 us
  local copies, waits for them, and re-layouts: 5.12 us -> 3.05 us
    pallas_call x1, Pallas kernels: 91.1 us -> 83.9 us  [on_device(): pl.pallas_call(kernel, out_shape=(block, block), in_specs=[pl.BlockSpec(m...]
    unnamed x10 -> x4, local copies, waits for them, and re-layouts: 5.12 us -> 3.05 us
where the time goes in v3:
time: 88.6 us; the launch traced here: 87.6 us
  Pallas kernels  83.9 us (95%)
  local copies, waits for them, and re-layouts  3.05 us (3%)
    pallas_call x1, Pallas kernels, on_device(): pl.pallas_call(kernel, out_shape=(block, block), in_specs=[pl.BlockSpec(m...  83.9 us
    unnamed x4, local copies, waits for them, and re-layouts  3.05 us

profile of v3, /device:TPU:0, one launch (start us, length us, event | category | flops | bytes accessed | tf_op | source)
XLA Modules:
  0.0 87.6 jit_solution(8375633887535959675)
XLA Ops:
  0.6 83.9 %shard_map.86 = (f32[1536,128]{1,0:T(8,128)}, f32[1536,128]{1,0:T(8,128)}) custom-call(s32[32]{0:T(128)} %owner.1, s32[6,32]{1,0:T(8,128)} %bitcast.12, s32[6,32]{1,0:T(8,128)} %bitcast.13, f32[3,6,6]{2,1,0:T(8,128)} %mats.1, f32[384,128]{1,0:T(8,128)} %bitcast.10, f32[1536,128]{1,0:T(8,128)} %bitcast.9, f32[256,128]{1,0:T(8,128)} %bitcast.11), custom_call_target="tpu_custom_call" | custom-call | tf_op jit(solution)/shard_map/pallas_call | solution.py:715
  84.5 0.0 copy-start
  84.5 2.2 %copy.11 = f32[1,1,6,16,16,128]{5,4,3,2,1,0:T(8,128)} copy(f32[1,1,6,16,16,128]{5,4,3,2,1,0:T(8,128)} %bitcast.8) | data formatting | bytes 1572864
  86.7 0.0 copy-done
  86.7 0.9 %copy.12 = f32[1,6,16,16,128]{4,3,2,1,0:T(8,128)} copy(f32[1,6,16,16,128]{4,3,2,1,0:T(8,128)S(1)} %bitcast.7) | data formatting | bytes 1572864
Async XLA Ops:
  84.5 2.2 %copy-start = (f32[1536,128]{1,0:T(8,128)S(1)}, f32[1536,128]{1,0:T(8,128)}, u32[]{:S(2)}) copy-start(f32[1536,128]{1,0:T(8,128)} %get-tuple-element.5) | copy-start | bytes 2359300

commit v4 on v3

--- a/solution.py
+++ b/solution.py
@@ -306,15 +306,18 @@
     tau = (0.5 * TAU) * rate[rows_of(x * CY, CY), :]
     new = [u[v] - tau * total[v] - DAMP * jnp.tanh(u[v]) for v in range(NV)]
     for v in range(NV):
-        out[cell_rows(v, x), :] = new[v]
-    pack_z(new, x, pa, pb)
-
-
-def adjoint_step(mats, rate, grid, wgrid, lam, out, x, final=None, weighted=None, pa=None, pb=None):
+        if pa is None:
+            out[rows_of(v * 256 + x * CY, CY), :] = new[v]
+        else:
+            out[cell_rows(v, x), :] = new[v]
+    if pa is not None:
+        pack_z(new, x, pa, pb)
+
+
+def adjoint_step(mats, rate, grid, wgrid, lam, out, x, weighted=None, pa=None, pb=None):
     u, at_u = neighbours_of(grid, x)
     w, at_w = neighbours_of(wgrid, x)
     total = [jnp.zeros((CY, CZ), F32) for _ in range(NV)]
-    flux = [jnp.zeros((CY, CZ), F32) for _ in range(NV)]
     tilt = jnp.zeros((CY, CZ), F32)
     for d in range(3):
         up, low = at_u(d)
@@ -323,7 +326,6 @@
         sl, rl = spread_of(u[0], low[0])
         dot_u = jnp.zeros((CY, CZ), F32)
         dot_l = jnp.zeros((CY, CZ), F32)
-        diff = []
         wdiff = []
         for i in range(NV):
             du, dl = up[i] - u[i], u[i] - low[i]
@@ -332,21 +334,12 @@
             dot_l = dot_l + dl * gl
             total[i] = total[i] + (su * gu - sl * gl)
             wdiff.append(wup[i] - wlow[i])
-            if final is not None:
-                flux[i] = flux[i] - (su * du - sl * dl)
-                diff.append(up[i] - low[i])
         tilt = tilt + ru * dot_u + rl * dot_l
         for i in range(NV):
             acc = total[i]
             for j in range(NV):
                 acc = acc + mats[d, j, i] * wdiff[j]
             total[i] = acc
-        if final is not None:
-            for i in range(NV):
-                acc = flux[i]
-                for j in range(NV):
-                    acc = acc + mats[d, i, j] * diff[j]
-                flux[i] = acc
     tau = TAU * rate[rows_of(x * CY, CY), :]
     packed = []
     for v in range(NV):
@@ -357,11 +350,10 @@
         if v == 0:
             new = new - 0.25 * tilt
         out[here, :] = new
-        if final is not None:
-            final[here, :] = u[v] - (0.5 * tau) * flux[v] - DAMP * bent
+        if weighted is not None:
             packed.append(tau * new)
             weighted[cell_rows(v, x), :] = packed[v]
-    if final is not None:
+    if weighted is not None:
         pack_z(packed, x, pa, pb)
 
 
@@ -444,17 +436,23 @@
 
 RING = NX
 HOPS = (2, 1, 3)
-N_COPIES = 2 + 6 * len(HOPS)
+N_COPIES = 1 + 3 * len(HOPS)
 
 
 class Exchange:
-    def __init__(self, place, bufs, outs, arrivals, send, recv, base):
-        self.place, self.bufs, self.outs, self.arrivals = place, bufs, outs, arrivals
+    def __init__(self, place, parts, scratch, send, recv, base):
+        self.place, self.parts = place, parts
+        self.bufs, self.outs, self.arrivals = (
+            dict(zip(parts, scratch[n::3])) for n in range(3)
+        )
         self.send, self.recv, self.base = send, recv, base
         self.all = []
         self.first = {"A": place.along_x, "B": place.along_y}
         self.second = {"A": place.along_y, "B": place.along_x}
-        self.across, self.own, self.passed, self.final = {}, {}, {}, {}
+        self.across = {}
+        self.own = {part: [] for part in parts}
+        self.passed = {part: [] for part in parts}
+        self.final = {part: [] for part in parts}
 
     def copy(self, src, dst, device):
         n = self.base + len(self.all)
@@ -470,63 +468,73 @@
         self.all.append(made)
         return made
 
-    def send_across(self, halves="AB"):
-        for half in halves:
-            buf = self.bufs[half]
-            self.across[half] = self.copy(buf.at[0], buf.at[RING], self.place.across_z())
-
-    def send_own(self, halves="AB"):
-        for half in halves:
-            self.own[half] = []
-        for k in HOPS:
-            for half in halves:
-                buf = self.bufs[half]
-                self.own[half].append(self.copy(buf.at[0], buf.at[k], self.first[half](k)))
+    def send_across(self, parts=None):
+        for part in parts or self.parts:
+            buf = self.bufs[part]
+            self.across[part] = self.copy(buf.at[0], buf.at[RING], self.place.across_z())
+
+    def send_own(self, parts=None):
+        for part in parts or self.parts:
+            buf, away = self.bufs[part], self.first[part[0]]
+            for k in HOPS:
+                self.own[part].append(self.copy(buf.at[0], buf.at[k], away(k)))
 
     def relay(self):
-        self.passed = {"A": [], "B": []}
-        for half in "AB":
-            self.across[half].wait_recv()
-        for k in HOPS:
-            for half in "AB":
-                buf = self.bufs[half]
-                self.passed[half].append(self.copy(buf.at[RING], buf.at[RING + k], self.first[half](k)))
+        for part in self.parts:
+            buf, away = self.bufs[part], self.first[part[0]]
+            self.across[part].wait_recv()
+            for k in HOPS:
+                self.passed[part].append(self.copy(buf.at[RING], buf.at[RING + k], away(k)))
 
     def hand_on(self, tables, segments):
-        self.final = {"A": [], "B": []}
-        for half in "AB":
-            for made in self.own[half] + self.passed[half]:
+        for part in self.parts:
+            for made in self.own[part] + self.passed[part]:
                 made.wait_recv()
-            buf, out, arrive = self.bufs[half], self.outs[half], self.arrivals[half]
+            buf, out, arrive = self.bufs[part], self.outs[part], self.arrivals[part]
             for k in HOPS + (0,):
-                for start, count, layer in segments[half]:
-                    picked = buf[tables.slot(half, k, layer), pl.ds(start, count), :]
+                for start, count, layer in segments[part]:
+                    picked = buf[tables.slot(part[0], k, layer), pl.ds(start, count), :]
                     if k == 0:
                         arrive[0, pl.ds(start, count), :] = picked
                     else:
                         out[k - 1, pl.ds(start, count), :] = picked
                 if k:
-                    self.final[half].append(
-                        self.copy(out.at[k - 1], arrive.at[k], self.second[half](k))
+                    self.final[part].append(
+                        self.copy(out.at[k - 1], arrive.at[k], self.second[part[0]](k))
                     )
 
     def take(self, tables, segments, put):
-        for half in "AB":
-            for made in self.final[half]:
+        for part in self.parts:
+            for made in self.final[part]:
                 made.wait_recv()
-            for start, count, layer in segments[half]:
-                put(half, start, count, self.arrivals[half][tables.last(half, layer), pl.ds(start, count), :])
+            arrive = self.arrivals[part]
+            for start, count, layer in segments[part]:
+                put(part, start, count, arrive[tables.last(part[0], layer), pl.ds(start, count), :])
 
     def drain(self):
         for made in self.all:
             made.wait_send()
 
 
+WHOLES = ("A1", "B1", "A2", "B2")
+BIG = FACE + CY
+
+
 def full_segments():
     return {
-        "A": [(s, n, f) for (s, n), f in zip(SEGS, (0, 1, 4))],
-        "B": [(s, n, f) for (s, n), f in zip(SEGS, (2, 3, 5))],
+        "A1": [(0, FACE, 0), (FACE, CY, 4)],
+        "B1": [(0, FACE, 2), (FACE, CY, 5)],
+        "A2": [(0, FACE, 1)],
+        "B2": [(0, FACE, 3)],
     }
+
+
+def whole_packet(pa, pb, exchange):
+    for source, name in ((pa, "A"), (pb, "B")):
+        one, two = exchange.bufs[name + "1"], exchange.bufs[name + "2"]
+        one[0, pl.ds(0, FACE), :] = source[pl.ds(0, FACE), :]
+        one[0, pl.ds(FACE, CY), :] = source[pl.ds(2 * FACE, CY), :]
+        two[0, pl.ds(0, FACE), :] = source[pl.ds(FACE, FACE), :]
 
 
 def quarter_segments(c):
@@ -544,20 +552,12 @@
     }
 
 
-def exchange_scratch(ra, rb):
-    return [
-        VMEM((2 * RING, ra, CZ), F32),
-        VMEM((2 * RING, rb, CZ), F32),
-        VMEM((RING - 1, ra, CZ), F32),
-        VMEM((RING - 1, rb, CZ), F32),
-        VMEM((RING, ra, CZ), F32),
-        VMEM((RING, rb, CZ), F32),
-    ]
-
-
-def exchange_of(place, scratch, send, recv, base):
-    ba, bb, oa, ob, ra, rb = scratch
-    return Exchange(place, {"A": ba, "B": bb}, {"A": oa, "B": ob}, {"A": ra, "B": rb}, send, recv, base)
+def exchange_scratch(*rows):
+    made = []
+    for r in rows:
+        for slots in (2 * RING, RING - 1, RING):
+            made.append(VMEM((slots, r, CZ), F32))
+    return made
 
 
 def quarter_packet(c, pa, pb, ba, bb):
@@ -597,35 +597,37 @@
 
 def put_halves(wa, wb):
     def put(half, start, count, value):
-        (wa if half == "A" else wb)[pl.ds(start, count), :] = value
+        at = FACE if half[1] == "2" else 2 * start
+        (wa if half[0] == "A" else wb)[pl.ds(at, count), :] = value
 
     return put
 
 
 def kernel(owner, links, codes, mats, part, seeds, rate, adjoint, final, *scratch):
     first, second = scratch[0:6], scratch[6:12]
-    third, fourth = scratch[12:18], scratch[18:24]
-    grid0, grid1, wgrid, wgrid1 = (scratch[24 + 3 * n : 27 + 3 * n] for n in range(4))
-    pa, pb, mine, mine1, stored, landed, landed1, wa, wb, lam, xface, xshare, send, recv = scratch[36:]
+    third, fourth = scratch[12:24], scratch[24:36]
+    scratch = scratch[36:]
+    grid0, grid1, wgrid, wgrid1 = (scratch[3 * n : 3 * n + 3] for n in range(4))
+    pa, pb, mine, mine1, stored, landed, landed1, wa, wb, lam, xface, xshare, send, recv = scratch[12:]
     place = Place()
-    early = exchange_of(place, first, send, recv, 0)
-    late = exchange_of(place, third, send, recv, N_COPIES)
-    again = exchange_of(place, second, send, recv, 2 * N_COPIES)
-    back = exchange_of(place, fourth, send, recv, 3 * N_COPIES)
-    base = 4 * N_COPIES
+    early = Exchange(place, "AB", first, send, recv, 0)
+    again = Exchange(place, "AB", second, send, recv, 2 * N_COPIES)
+    late = Exchange(place, WHOLES, third, send, recv, 4 * N_COPIES)
+    back = Exchange(place, WHOLES, fourth, send, recv, 8 * N_COPIES)
+    base = 12 * N_COPIES
     gather = Gather(place, part, stored, send, recv, base + 6)
     ends = EndLayers(place, xface, xshare, send, recv, base + 9)
     strips, quarters, wholes = strip_segments(), quarter_segments(place.c), full_segments()
 
     met = greet(place, True)
-    pack_strip(part, place.c, xface, first[0], first[1])
+    pack_strip(part, place.c, xface, early.bufs["A"], early.bufs["B"])
     met()
     ends.begin()
     early.send_across("B")
     early.send_own("B")
     ends.take()
     for n in range(2):
-        first[0][0, pl.ds(n * QROW, QROW), :] = xshare[n]
+        early.bufs["A"][0, pl.ds(n * QROW, QROW), :] = xshare[n]
     early.send_across("A")
     early.send_own("A")
     gather.begin()
@@ -641,8 +643,7 @@
 
     each_x(weigh)
     pack_xy(wgrid[0], pa, pb)
-    third[0][0] = pa[...]
-    third[1][0] = pb[...]
+    whole_packet(pa, pb, late)
     early.relay()
     late.send_across()
     tables = Tables(place, owner, links)
@@ -666,7 +667,7 @@
     each_x(lambda x: forward_step(mats, rate, grid0, grid1[0], pa, pb, x))
     pack_xy(grid1[0], pa, pb)
 
-    quarter_packet(place.c, pa, pb, second[0], second[1])
+    quarter_packet(place.c, pa, pb, again.bufs["A"], again.bufs["B"])
     again.send_across()
     again.send_own()
     again.relay()
@@ -682,17 +683,22 @@
     place_ghosts(forward_layers(landed1), code, *grid1)
 
     def middle(x):
-        adjoint_step(mats, rate, grid1, wgrid, seeds, lam, x, final, wgrid1[0], pa, pb)
+        adjoint_step(mats, rate, grid1, wgrid, seeds, lam, x, wgrid1[0], pa, pb)
 
     each_x(middle)
     pack_xy(wgrid1[0], pa, pb)
 
-    fourth[0][0] = pa[...]
-    fourth[1][0] = pb[...]
+    whole_packet(pa, pb, back)
     back.send_across()
     back.send_own()
+    def last(x):
+        forward_step(mats, rate, grid1, final, None, None, x)
+
+    each_x(last, 0, 6)
     back.relay()
+    each_x(last, 6, 10)
     back.hand_on(tables, wholes)
+    each_x(last, 10, CX)
     back.take(tables, wholes, put_halves(wa, wb))
     place_ghosts(adjoint_layers(wa, wb), code, *wgrid1)
     each_x(lambda x: adjoint_step(mats, rate, grid0, wgrid1, lam, adjoint, x))
@@ -708,10 +714,10 @@
     vm, sm = pltpu.VMEM, pltpu.SMEM
     block = jax.ShapeDtypeStruct((ROWS, CZ), F32)
     strip, quarter = exchange_scratch(QX, QX), exchange_scratch(QA, QB)
-    whole = exchange_scratch(HALF, HALF)
+    whole = exchange_scratch(BIG, BIG, FACE, FACE)
     grid = [VMEM((NV * EXT, CZ), F32), VMEM((2 * FACE, CZ), F32), VMEM((2 * CY, CZ), F32)]
     half = VMEM((HALF, CZ), F32)
-    copies = 17 + 4 * N_COPIES
+    copies = 17 + 12 * N_COPIES
     adjoint, final = pl.pallas_call(
         kernel,
         out_shape=(block, block),

time: 88.6 us -> 84.5 us (0.954)
  Pallas kernels: 83.9 us -> 80.4 us
    pallas_call x1, Pallas kernels: 83.9 us -> 80.4 us  [on_device(): pl.pallas_call(kernel, out_shape=(block, block), in_specs=[pl.BlockSpec(m...]
where the time goes in v4:
time: 84.5 us; the launch traced here: 84.1 us
  Pallas kernels  80.4 us (95%)
  local copies, waits for them, and re-layouts  3.05 us (4%)
    pallas_call x1, Pallas kernels, on_device(): pl.pallas_call(kernel, out_shape=(block, block), in_specs=[pl.BlockSpec(m...  80.4 us
    unnamed x4, local copies, waits for them, and re-layouts  3.05 us

profile of v4, /device:TPU:0, one launch (start us, length us, event | category | flops | bytes accessed | tf_op | source)
XLA Modules:
  0.0 84.1 jit_solution(12872757124152831151)
XLA Ops:
  0.6 80.4 %shard_map.86 = (f32[1536,128]{1,0:T(8,128)}, f32[1536,128]{1,0:T(8,128)}) custom-call(s32[32]{0:T(128)} %owner.1, s32[6,32]{1,0:T(8,128)} %bitcast.12, s32[6,32]{1,0:T(8,128)} %bitcast.13, f32[3,6,6]{2,1,0:T(8,128)} %mats.1, f32[384,128]{1,0:T(8,128)} %bitcast.10, f32[1536,128]{1,0:T(8,128)} %bitcast.9, f32[256,128]{1,0:T(8,128)} %bitcast.11), custom_call_target="tpu_custom_call" | custom-call | tf_op jit(solution)/shard_map/pallas_call | solution.py:721
  81.1 0.0 copy-start
  81.1 2.2 %copy.11 = f32[1,1,6,16,16,128]{5,4,3,2,1,0:T(8,128)} copy(f32[1,1,6,16,16,128]{5,4,3,2,1,0:T(8,128)} %bitcast.8) | data formatting | bytes 1572864
  83.3 0.0 copy-done
  83.3 0.9 %copy.12 = f32[1,6,16,16,128]{4,3,2,1,0:T(8,128)} copy(f32[1,6,16,16,128]{4,3,2,1,0:T(8,128)S(1)} %bitcast.7) | data formatting | bytes 1572864
Async XLA Ops:
  81.1 2.2 %copy-start = (f32[1536,128]{1,0:T(8,128)S(1)}, f32[1536,128]{1,0:T(8,128)}, u32[]{:S(2)}) copy-start(f32[1536,128]{1,0:T(8,128)} %get-tuple-element.5) | copy-start | bytes 2359300

commit v5 on v4

--- a/solution.py
+++ b/solution.py
@@ -254,7 +254,7 @@
     return layer
 
 
-def neighbours_of(grid, x):
+def neighbours_of(grid, x, stand=None):
     ext, gy, gz = grid
     row = lax.broadcasted_iota(jnp.int32, (CY, CZ), 0)
     lane = lanes((CY, CZ))
@@ -268,6 +268,12 @@
             if direction == 0:
                 up = ext[cell_rows(v, x + 1), :]
                 low = ext[cell_rows(v, x - 1), :]
+            elif stand is not None:
+                axis, size = direction - 1, (CY, CZ)[direction - 1]
+                at_side = (row, lane)[axis]
+                other = u if stand == "own" else jnp.zeros_like(u)
+                up = jnp.where(at_side == size - 1, other, pltpu.roll(u, size - 1, axis))
+                low = jnp.where(at_side == 0, other, pltpu.roll(u, 1, axis))
             elif direction == 1:
                 up = jnp.where(row == CY - 1, gy[pl.ds(at_x, 1), :], pltpu.roll(u, CY - 1, 0))
                 low = jnp.where(row == 0, gy[pl.ds(FACE + at_x, 1), :], pltpu.roll(u, 1, 0))
@@ -290,8 +296,8 @@
     return t * r, mean * r
 
 
-def forward_step(mats, rate, grid, out, pa, pb, x):
-    u, at = neighbours_of(grid, x)
+def forward_step(mats, rate, grid, out, pa, pb, x, stand=None):
+    u, at = neighbours_of(grid, x, stand)
     total = [jnp.zeros((CY, CZ), F32) for _ in range(NV)]
     for d in range(3):
         up, low = at(d)
@@ -311,12 +317,12 @@
         else:
             out[cell_rows(v, x), :] = new[v]
     if pa is not None:
-        pack_z(new, x, pa, pb)
-
-
-def adjoint_step(mats, rate, grid, wgrid, lam, out, x, weighted=None, pa=None, pb=None):
+        pack_z(new if stand is None else u, x, pa, pb)
+
+
+def adjoint_step(mats, rate, grid, wgrid, lam, out, x, weighted=None, pa=None, pb=None, stand=None):
     u, at_u = neighbours_of(grid, x)
-    w, at_w = neighbours_of(wgrid, x)
+    w, at_w = neighbours_of(wgrid, x, stand)
     total = [jnp.zeros((CY, CZ), F32) for _ in range(NV)]
     tilt = jnp.zeros((CY, CZ), F32)
     for d in range(3):
@@ -357,6 +363,91 @@
         pack_z(packed, x, pa, pb)
 
 
+def own_tile(f, v, pa, pb):
+    half = (pa, pa, pb, pb, pa, pb)[f]
+    if f < 4:
+        return half[pl.ds((f % 2) * FACE + v * 16, 16), :]
+    return pltpu.roll(half[pl.ds(2 * FACE, CY), :], (CZ - v * 16) % CZ, 1)
+
+
+def ghost_tile(f, v, grid):
+    ext, gy, gz = grid
+    if f < 2:
+        return ext[pl.ds(v * EXT + ((CX + 1) * CY if f == 0 else 0), CY), :]
+    if f < 4:
+        return gy[pl.ds((f - 2) * FACE + v * 16, 16), :]
+    return pltpu.roll(gz[pl.ds((f - 4) * CY, CY), :], (CZ - v * 16) % CZ, 1)
+
+
+def forward_fix(f, mats, grid, pa, pb):
+    sign = -0.5 if f % 2 == 0 else 0.5
+    own = [own_tile(f, v, pa, pb) for v in range(NV)]
+    across = [ghost_tile(f, v, grid) for v in range(NV)]
+    delta = [g - u for g, u in zip(across, own)]
+    spread, _ = spread_of(across[0], own[0])
+    fixes = []
+    for i in range(NV):
+        acc = mats[f // 2, i, 0] * delta[0]
+        for j in range(1, NV):
+            acc = acc + mats[f // 2, i, j] * delta[j]
+        fixes.append(sign * acc + 0.5 * spread * delta[i])
+    return fixes
+
+
+def adjoint_fix(f, mats, grid, wgrid, pa, pb):
+    sign = 0.5 if f % 2 == 0 else -0.5
+    own = [own_tile(f, v, pa, pb) for v in range(NV)]
+    across = [ghost_tile(f, v, grid) for v in range(NV)]
+    w = [ghost_tile(f, v, wgrid) for v in range(NV)]
+    spread, ratio = spread_of(across[0], own[0])
+    dot = jnp.zeros((CY, CZ), F32)
+    for i in range(NV):
+        dot = dot + (across[i] - own[i]) * w[i]
+    fixes = []
+    for i in range(NV):
+        acc = mats[f // 2, 0, i] * w[0]
+        for j in range(1, NV):
+            acc = acc + mats[f // 2, j, i] * w[j]
+        fixes.append(sign * acc + 0.5 * spread * w[i])
+    fixes[0] = fixes[0] - 0.25 * ratio * dot
+    return fixes
+
+
+def repair(fix, out, stride, offset, fz, rate=None, pa=None, pb=None):
+    for f in range(4):
+        fixes = fix(f)
+        first = f % 2 == 1
+        if f < 2:
+            x = 0 if first else CX - 1
+            tau = None if rate is None else TAU * rate[pl.ds(x * CY, CY), :]
+            rows = [pl.ds(v * stride + offset + x * CY, CY) for v in range(NV)]
+        else:
+            y = 0 if first else CY - 1
+            tau = None if rate is None else TAU * rate[pl.ds(y, CX, stride=CY), :]
+            rows = [pl.ds(v * stride + offset + y, CX, stride=CY) for v in range(NV)]
+        for v in range(NV):
+            out[rows[v], :] = out[rows[v], :] + (fixes[v] if tau is None else tau * fixes[v])
+    for f in (4, 5):
+        for v, value in enumerate(fix(f)):
+            fz[pl.ds(((f - 4) * NV + v) * CY, CY), :] = value
+    lane = lanes((CY, CZ))
+
+    def sides(x):
+        tau = None if rate is None else TAU * rate[rows_of(x * CY, CY), :]
+        values = []
+        for v in range(NV):
+            up = pltpu.roll(fz[pl.ds(v * CY, CY), :], CZ - 1 - x, 1)
+            low = pltpu.roll(fz[pl.ds((NV + v) * CY, CY), :], lax.rem(CZ - x, CZ), 1)
+            add = jnp.where(lane == CZ - 1, up, jnp.where(lane == 0, low, 0.0))
+            here = rows_of(v * stride + offset + x * CY, CY)
+            values.append(out[here, :] + (add if tau is None else tau * add))
+            out[here, :] = values[v]
+        if pa is not None:
+            pack_z(values, x, pa, pb)
+
+    each_x(sides)
+
+
 def each_x(step, start=0, stop=CX):
     def body(x, carry):
         step(x)
@@ -608,7 +699,7 @@
     third, fourth = scratch[12:24], scratch[24:36]
     scratch = scratch[36:]
     grid0, grid1, wgrid, wgrid1 = (scratch[3 * n : 3 * n + 3] for n in range(4))
-    pa, pb, mine, mine1, stored, landed, landed1, wa, wb, lam, xface, xshare, send, recv = scratch[12:]
+    pa, pb, mine, mine1, stored, landed, landed1, wa, wb, lam, xface, xshare, pu, pw, fz, send, recv = scratch[12:]
     place = Place()
     early = Exchange(place, "AB", first, send, recv, 0)
     again = Exchange(place, "AB", second, send, recv, 2 * N_COPIES)
@@ -658,13 +749,20 @@
     for c in range(NC):
         for v in range(NV):
             grid0[0][pl.ds(v * EXT + CY + c * span, span), :] = stored[c, pl.ds(v * span, span), :]
+    for v in range(NV):
+        for ghost, x in ((0, 0), (CX + 1, CX - 1)):
+            grid0[0][pl.ds(v * EXT + ghost * CY, CY), :] = grid0[0][pl.ds(v * EXT + (x + 1) * CY, CY), :]
+    clear_z(pu, pw)
+    pack_xy(grid0[0], pu, pw)
+    late.relay()
+    each_x(lambda x: forward_step(mats, rate, grid0, grid1[0], pu, pw, x, "own"))
     clear_z(pa, pb)
-    late.relay()
     for copy in shared:
         copy.wait_recv()
     place_ghosts(strip_layers(landed), code, *grid0)
-
-    each_x(lambda x: forward_step(mats, rate, grid0, grid1[0], pa, pb, x))
+    repair(
+        lambda f: forward_fix(f, mats, grid0, pu, pw), grid1[0], EXT, CY, fz, rate, pa, pb
+    )
     pack_xy(grid1[0], pa, pb)
 
     quarter_packet(place.c, pa, pb, again.bufs["A"], again.bufs["B"])
@@ -694,14 +792,22 @@
     def last(x):
         forward_step(mats, rate, grid1, final, None, None, x)
 
-    each_x(last, 0, 6)
+    for v in range(NV):
+        for ghost in (0, CX + 1):
+            wgrid1[0][pl.ds(v * EXT + ghost * CY, CY), :] = jnp.zeros((CY, CZ), F32)
+
+    def end(x):
+        adjoint_step(mats, rate, grid0, wgrid1, lam, adjoint, x, stand="zero")
+
+    each_x(last, 0, 10)
     back.relay()
-    each_x(last, 6, 10)
+    each_x(last, 10, CX)
+    each_x(end, 0, 4)
     back.hand_on(tables, wholes)
-    each_x(last, 10, CX)
+    each_x(end, 4, CX)
     back.take(tables, wholes, put_halves(wa, wb))
     place_ghosts(adjoint_layers(wa, wb), code, *wgrid1)
-    each_x(lambda x: adjoint_step(mats, rate, grid0, wgrid1, lam, adjoint, x))
+    repair(lambda f: adjoint_fix(f, mats, grid0, wgrid1, pu, pw), adjoint, CX * CY, 0, fz)
 
     for copy in shared + shared1:
         copy.wait_send()
@@ -731,6 +837,7 @@
         + [VMEM((NC, ROWS // NC, CZ), F32)]
         + [VMEM((NC, 2 * QX, CZ), F32), VMEM((NC, QA + QB, CZ), F32), half, half]
         + [VMEM((ROWS, CZ), F32), VMEM((2, FACE, CZ), F32), VMEM((2, QROW, CZ), F32)]
+        + [half, half, VMEM((2 * NV * CY, CZ), F32)]
         + [pltpu.SemaphoreType.DMA((copies,)), pltpu.SemaphoreType.DMA((copies,))],
         compiler_params=pltpu.CompilerParams(collective_id=0, has_side_effects=True),
     )(

time: 84.5 us -> 81.3 us (0.962)
  Pallas kernels: 80.4 us -> 77.2 us
    pallas_call x1, Pallas kernels: 80.4 us -> 77.2 us  [on_device(): pl.pallas_call(kernel, out_shape=(block, block), in_specs=[pl.BlockSpec(m...]
where the time goes in v5:
time: 81.3 us; the launch traced here: 80.9 us
  Pallas kernels  77.2 us (95%)
  local copies, waits for them, and re-layouts  3.05 us (4%)
    pallas_call x1, Pallas kernels, on_device(): pl.pallas_call(kernel, out_shape=(block, block), in_specs=[pl.BlockSpec(m...  77.2 us
    unnamed x4, local copies, waits for them, and re-layouts  3.05 us

profile of v5, /device:TPU:0, one launch (start us, length us, event | category | flops | bytes accessed | tf_op | source)
XLA Modules:
  0.0 80.9 jit_solution(5362667190408820342)
XLA Ops:
  0.6 77.2 %shard_map.86 = (f32[1536,128]{1,0:T(8,128)}, f32[1536,128]{1,0:T(8,128)}) custom-call(s32[32]{0:T(128)} %owner.1, s32[6,32]{1,0:T(8,128)} %bitcast.12, s32[6,32]{1,0:T(8,128)} %bitcast.13, f32[3,6,6]{2,1,0:T(8,128)} %mats.1, f32[384,128]{1,0:T(8,128)} %bitcast.10, f32[1536,128]{1,0:T(8,128)} %bitcast.9, f32[256,128]{1,0:T(8,128)} %bitcast.11), custom_call_target="tpu_custom_call" | custom-call | tf_op jit(solution)/shard_map/pallas_call | solution.py:827
  77.8 0.0 copy-start
  77.9 2.2 %copy.11 = f32[1,1,6,16,16,128]{5,4,3,2,1,0:T(8,128)} copy(f32[1,1,6,16,16,128]{5,4,3,2,1,0:T(8,128)} %bitcast.8) | data formatting | bytes 1572864
  80.0 0.0 copy-done
  80.0 0.9 %copy.12 = f32[1,6,16,16,128]{4,3,2,1,0:T(8,128)} copy(f32[1,6,16,16,128]{4,3,2,1,0:T(8,128)S(1)} %bitcast.7) | data formatting | bytes 1572864
Async XLA Ops:
  77.8 2.2 %copy-start = (f32[1536,128]{1,0:T(8,128)S(1)}, f32[1536,128]{1,0:T(8,128)}, u32[]{:S(2)}) copy-start(f32[1536,128]{1,0:T(8,128)} %get-tuple-element.5) | copy-start | bytes 2359300

commit v6 on v5

--- a/solution.py
+++ b/solution.py
@@ -16,6 +16,7 @@
 EXT = (CX + 2) * CY
 TAU = 0.05
 DAMP = 0.015
+M0, M1, M2 = 5, 6, 10
 HALF = 2 * FACE + CY
 QROW = FACE // NC
 QA, QB = 2 * QROW + 8, 2 * QROW
@@ -320,9 +321,9 @@
         pack_z(new if stand is None else u, x, pa, pb)
 
 
-def adjoint_step(mats, rate, grid, wgrid, lam, out, x, weighted=None, pa=None, pb=None, stand=None):
-    u, at_u = neighbours_of(grid, x)
-    w, at_w = neighbours_of(wgrid, x, stand)
+def adjoint_step(mats, grid, wgrid, lam, out, x, stand=None):
+    u, at_u = neighbours_of(grid, x, stand)
+    w, at_w = neighbours_of(wgrid, x, "zero")
     total = [jnp.zeros((CY, CZ), F32) for _ in range(NV)]
     tilt = jnp.zeros((CY, CZ), F32)
     for d in range(3):
@@ -346,8 +347,6 @@
             for j in range(NV):
                 acc = acc + mats[d, j, i] * wdiff[j]
             total[i] = acc
-    tau = TAU * rate[rows_of(x * CY, CY), :]
-    packed = []
     for v in range(NV):
         here = rows_of(v * 256 + x * CY, CY)
         bent = jnp.tanh(u[v])
@@ -356,11 +355,6 @@
         if v == 0:
             new = new - 0.25 * tilt
         out[here, :] = new
-        if weighted is not None:
-            packed.append(tau * new)
-            weighted[cell_rows(v, x), :] = packed[v]
-    if weighted is not None:
-        pack_z(packed, x, pa, pb)
 
 
 def own_tile(f, v, pa, pb):
@@ -377,6 +371,12 @@
     if f < 4:
         return gy[pl.ds((f - 2) * FACE + v * 16, 16), :]
     return pltpu.roll(gz[pl.ds((f - 4) * CY, CY), :], (CZ - v * 16) % CZ, 1)
+
+
+def own_planes(ext):
+    for v in range(NV):
+        for ghost, x in ((0, 0), (CX + 1, CX - 1)):
+            ext[pl.ds(v * EXT + ghost * CY, CY), :] = ext[pl.ds(v * EXT + (x + 1) * CY, CY), :]
 
 
 def forward_fix(f, mats, grid, pa, pb):
@@ -394,26 +394,35 @@
     return fixes
 
 
-def adjoint_fix(f, mats, grid, wgrid, pa, pb):
+def adjoint_fix(f, mats, grid, wgrid, pa, pb, qa=None, qb=None):
     sign = 0.5 if f % 2 == 0 else -0.5
     own = [own_tile(f, v, pa, pb) for v in range(NV)]
     across = [ghost_tile(f, v, grid) for v in range(NV)]
     w = [ghost_tile(f, v, wgrid) for v in range(NV)]
     spread, ratio = spread_of(across[0], own[0])
+    if qa is None:
+        jump, kept = w, None
+    else:
+        mine = [own_tile(f, v, qa, qb) for v in range(NV)]
+        jump = [a - b for a, b in zip(w, mine)]
+        kept, _ = spread_of(own[0], own[0])
     dot = jnp.zeros((CY, CZ), F32)
     for i in range(NV):
-        dot = dot + (across[i] - own[i]) * w[i]
+        dot = dot + (across[i] - own[i]) * jump[i]
     fixes = []
     for i in range(NV):
         acc = mats[f // 2, 0, i] * w[0]
         for j in range(1, NV):
             acc = acc + mats[f // 2, j, i] * w[j]
-        fixes.append(sign * acc + 0.5 * spread * w[i])
+        lean = spread * jump[i]
+        if kept is not None:
+            lean = lean + kept * mine[i]
+        fixes.append(sign * acc + 0.5 * lean)
     fixes[0] = fixes[0] - 0.25 * ratio * dot
     return fixes
 
 
-def repair(fix, out, stride, offset, fz, rate=None, pa=None, pb=None):
+def repair(fix, out, stride, offset, fz, rate=None, pa=None, pb=None, weighted=None, weight=None):
     for f in range(4):
         fixes = fix(f)
         first = f % 2 == 1
@@ -440,8 +449,12 @@
             low = pltpu.roll(fz[pl.ds((NV + v) * CY, CY), :], lax.rem(CZ - x, CZ), 1)
             add = jnp.where(lane == CZ - 1, up, jnp.where(lane == 0, low, 0.0))
             here = rows_of(v * stride + offset + x * CY, CY)
-            values.append(out[here, :] + (add if tau is None else tau * add))
-            out[here, :] = values[v]
+            value = out[here, :] + (add if tau is None else tau * add)
+            out[here, :] = value
+            if weighted is not None:
+                value = value * (TAU * weight[rows_of(x * CY, CY), :])
+                weighted[cell_rows(v, x), :] = value
+            values.append(value)
         if pa is not None:
             pack_z(values, x, pa, pb)
 
@@ -699,7 +712,7 @@
     third, fourth = scratch[12:24], scratch[24:36]
     scratch = scratch[36:]
     grid0, grid1, wgrid, wgrid1 = (scratch[3 * n : 3 * n + 3] for n in range(4))
-    pa, pb, mine, mine1, stored, landed, landed1, wa, wb, lam, xface, xshare, pu, pw, fz, send, recv = scratch[12:]
+    pa, pb, mine, mine1, stored, landed, landed1, wa, wb, lam, xface, xshare, pu, pw, qa, qb, fz, send, recv = scratch[12:]
     place = Place()
     early = Exchange(place, "AB", first, send, recv, 0)
     again = Exchange(place, "AB", second, send, recv, 2 * N_COPIES)
@@ -723,18 +736,22 @@
     early.send_own("A")
     gather.begin()
 
-    clear_z(pa, pb)
+    clear_z(qa, qb)
+    for v in range(NV):
+        for ghost in (0, CX + 1):
+            wgrid[0][pl.ds(v * EXT + ghost * CY, CY), :] = jnp.zeros((CY, CZ), F32)
+            wgrid1[0][pl.ds(v * EXT + ghost * CY, CY), :] = jnp.zeros((CY, CZ), F32)
 
     def weigh(x):
         tau = TAU * rate[rows_of(x * CY, CY), :]
         values = [seeds[rows_of(v * 256 + x * CY, CY), :] * tau for v in range(NV)]
         for v in range(NV):
             wgrid[0][cell_rows(v, x), :] = values[v]
-        pack_z(values, x, pa, pb)
+        pack_z(values, x, qa, qb)
 
     each_x(weigh)
-    pack_xy(wgrid[0], pa, pb)
-    whole_packet(pa, pb, late)
+    pack_xy(wgrid[0], qa, qb)
+    whole_packet(qa, qb, late)
     early.relay()
     late.send_across()
     tables = Tables(place, owner, links)
@@ -749,9 +766,7 @@
     for c in range(NC):
         for v in range(NV):
             grid0[0][pl.ds(v * EXT + CY + c * span, span), :] = stored[c, pl.ds(v * span, span), :]
-    for v in range(NV):
-        for ghost, x in ((0, 0), (CX + 1, CX - 1)):
-            grid0[0][pl.ds(v * EXT + ghost * CY, CY), :] = grid0[0][pl.ds(v * EXT + (x + 1) * CY, CY), :]
+    own_planes(grid0[0])
     clear_z(pu, pw)
     pack_xy(grid0[0], pu, pw)
     late.relay()
@@ -768,36 +783,47 @@
     quarter_packet(place.c, pa, pb, again.bufs["A"], again.bufs["B"])
     again.send_across()
     again.send_own()
+    own_planes(grid1[0])
+
+    def middle(x):
+        adjoint_step(mats, grid1, wgrid, seeds, lam, x, "own")
+
+    each_x(middle, 0, M0)
     again.relay()
     late.hand_on(tables, wholes)
+    each_x(middle, M0, M1)
     again.hand_on(tables, quarters)
+    each_x(middle, M1, M2)
     again.take(tables, quarters, put_into(mine1, QA))
     shared1 = share(place, mine1, landed1, send, recv, base + 3)
+    each_x(middle, M2, CX)
     late.take(tables, wholes, put_halves(wa, wb))
     place_ghosts(adjoint_layers(wa, wb), code, *wgrid)
-    clear_z(pa, pb)
     for copy in shared1:
         copy.wait_recv()
     place_ghosts(forward_layers(landed1), code, *grid1)
-
-    def middle(x):
-        adjoint_step(mats, rate, grid1, wgrid, seeds, lam, x, wgrid1[0], pa, pb)
-
-    each_x(middle)
-    pack_xy(wgrid1[0], pa, pb)
-
-    whole_packet(pa, pb, back)
+    repair(
+        lambda f: adjoint_fix(f, mats, grid1, wgrid, pa, pb, qa, qb),
+        lam,
+        CX * CY,
+        0,
+        fz,
+        pa=qa,
+        pb=qb,
+        weighted=wgrid1[0],
+        weight=rate,
+    )
+    pack_xy(wgrid1[0], qa, qb)
+
+    whole_packet(qa, qb, back)
     back.send_across()
     back.send_own()
+
     def last(x):
         forward_step(mats, rate, grid1, final, None, None, x)
 
-    for v in range(NV):
-        for ghost in (0, CX + 1):
-            wgrid1[0][pl.ds(v * EXT + ghost * CY, CY), :] = jnp.zeros((CY, CZ), F32)
-
     def end(x):
-        adjoint_step(mats, rate, grid0, wgrid1, lam, adjoint, x, stand="zero")
+        adjoint_step(mats, grid0, wgrid1, lam, adjoint, x)
 
     each_x(last, 0, 10)
     back.relay()
@@ -837,7 +863,7 @@
         + [VMEM((NC, ROWS // NC, CZ), F32)]
         + [VMEM((NC, 2 * QX, CZ), F32), VMEM((NC, QA + QB, CZ), F32), half, half]
         + [VMEM((ROWS, CZ), F32), VMEM((2, FACE, CZ), F32), VMEM((2, QROW, CZ), F32)]
-        + [half, half, VMEM((2 * NV * CY, CZ), F32)]
+        + [half, half, half, half, VMEM((2 * NV * CY, CZ), F32)]
         + [pltpu.SemaphoreType.DMA((copies,)), pltpu.SemaphoreType.DMA((copies,))],
         compiler_params=pltpu.CompilerParams(collective_id=0, has_side_effects=True),
     )(

time: 81.3 us -> 79 us (0.972)
  Pallas kernels: 77.2 us -> 75 us
    pallas_call x1, Pallas kernels: 77.2 us -> 75 us  [on_device(): pl.pallas_call(kernel, out_shape=(block, block), in_specs=[pl.BlockSpec(m...]
where the time goes in v6:
time: 79 us; the launch traced here: 78.7 us
  Pallas kernels  75 us (95%)
  local copies, waits for them, and re-layouts  3.05 us (4%)
    pallas_call x1, Pallas kernels, on_device(): pl.pallas_call(kernel, out_shape=(block, block), in_specs=[pl.BlockSpec(m...  75 us
    unnamed x4, local copies, waits for them, and re-layouts  3.05 us

profile of v6, /device:TPU:0, one launch (start us, length us, event | category | flops | bytes accessed | tf_op | source)
XLA Modules:
  0.0 78.7 jit_solution(6393432634131997683)
XLA Ops:
  0.6 75.0 %shard_map.86 = (f32[1536,128]{1,0:T(8,128)}, f32[1536,128]{1,0:T(8,128)}) custom-call(s32[32]{0:T(128)} %owner.1, s32[6,32]{1,0:T(8,128)} %bitcast.12, s32[6,32]{1,0:T(8,128)} %bitcast.13, f32[3,6,6]{2,1,0:T(8,128)} %mats.1, f32[384,128]{1,0:T(8,128)} %bitcast.10, f32[1536,128]{1,0:T(8,128)} %bitcast.9, f32[256,128]{1,0:T(8,128)} %bitcast.11), custom_call_target="tpu_custom_call" | custom-call | tf_op jit(solution)/shard_map/pallas_call | solution.py:853
  75.6 0.0 copy-start
  75.6 2.2 %copy.11 = f32[1,1,6,16,16,128]{5,4,3,2,1,0:T(8,128)} copy(f32[1,1,6,16,16,128]{5,4,3,2,1,0:T(8,128)} %bitcast.8) | data formatting | bytes 1572864
  77.8 0.0 copy-done
  77.8 0.9 %copy.12 = f32[1,6,16,16,128]{4,3,2,1,0:T(8,128)} copy(f32[1,6,16,16,128]{4,3,2,1,0:T(8,128)S(1)} %bitcast.7) | data formatting | bytes 1572864
Async XLA Ops:
  75.6 2.2 %copy-start = (f32[1536,128]{1,0:T(8,128)S(1)}, f32[1536,128]{1,0:T(8,128)}, u32[]{:S(2)}) copy-start(f32[1536,128]{1,0:T(8,128)} %get-tuple-element.5) | copy-start | bytes 2359300

commit v7 on v6

--- a/solution.py
+++ b/solution.py
@@ -790,12 +790,12 @@
 
     each_x(middle, 0, M0)
     again.relay()
-    late.hand_on(tables, wholes)
     each_x(middle, M0, M1)
     again.hand_on(tables, quarters)
     each_x(middle, M1, M2)
     again.take(tables, quarters, put_into(mine1, QA))
     shared1 = share(place, mine1, landed1, send, recv, base + 3)
+    late.hand_on(tables, wholes)
     each_x(middle, M2, CX)
     late.take(tables, wholes, put_halves(wa, wb))
     place_ghosts(adjoint_layers(wa, wb), code, *wgrid)

time: 79 us -> 76.1 us (0.963)
  Pallas kernels: 75 us -> 72.3 us
    pallas_call x1, Pallas kernels: 75 us -> 72.3 us  [on_device(): pl.pallas_call(kernel, out_shape=(block, block), in_specs=[pl.BlockSpec(m...]
where the time goes in v7:
time: 76.1 us; the launch traced here: 76 us
  Pallas kernels  72.3 us (95%)
  local copies, waits for them, and re-layouts  3.05 us (4%)
    pallas_call x1, Pallas kernels, on_device(): pl.pallas_call(kernel, out_shape=(block, block), in_specs=[pl.BlockSpec(m...  72.3 us
    unnamed x4, local copies, waits for them, and re-layouts  3.05 us

profile of v7, /device:TPU:0, one launch (start us, length us, event | category | flops | bytes accessed | tf_op | source)
XLA Modules:
  0.0 76.0 jit_solution(3447486225946968328)
XLA Ops:
  0.6 72.3 %shard_map.86 = (f32[1536,128]{1,0:T(8,128)}, f32[1536,128]{1,0:T(8,128)}) custom-call(s32[32]{0:T(128)} %owner.1, s32[6,32]{1,0:T(8,128)} %bitcast.12, s32[6,32]{1,0:T(8,128)} %bitcast.13, f32[3,6,6]{2,1,0:T(8,128)} %mats.1, f32[384,128]{1,0:T(8,128)} %bitcast.10, f32[1536,128]{1,0:T(8,128)} %bitcast.9, f32[256,128]{1,0:T(8,128)} %bitcast.11), custom_call_target="tpu_custom_call" | custom-call | tf_op jit(solution)/shard_map/pallas_call | solution.py:853
  72.9 0.0 copy-start
  72.9 2.2 %copy.11 = f32[1,1,6,16,16,128]{5,4,3,2,1,0:T(8,128)} copy(f32[1,1,6,16,16,128]{5,4,3,2,1,0:T(8,128)} %bitcast.8) | data formatting | bytes 1572864
  75.1 0.0 copy-done
  75.1 0.9 %copy.12 = f32[1,6,16,16,128]{4,3,2,1,0:T(8,128)} copy(f32[1,6,16,16,128]{4,3,2,1,0:T(8,128)S(1)} %bitcast.7) | data formatting | bytes 1572864
Async XLA Ops:
  72.9 2.2 %copy-start = (f32[1536,128]{1,0:T(8,128)S(1)}, f32[1536,128]{1,0:T(8,128)}, u32[]{:S(2)}) copy-start(f32[1536,128]{1,0:T(8,128)} %get-tuple-element.5) | copy-start | bytes 2359300

commit v8 on v7

--- a/solution.py
+++ b/solution.py
@@ -607,8 +607,8 @@
                         self.copy(out.at[k - 1], arrive.at[k], self.second[part[0]](k))
                     )
 
-    def take(self, tables, segments, put):
-        for part in self.parts:
+    def take(self, tables, segments, put, parts=None):
+        for part in parts or self.parts:
             for made in self.final[part]:
                 made.wait_recv()
             arrive = self.arrivals[part]
@@ -675,12 +675,12 @@
     ba[0, pl.ds(2 * QROW, 8), :] = jnp.where(c < 2, pa[zrows, :], pb[zrows, :])
 
 
-def share(place, mine, ghost, send, recv, base):
+def share(place, mine, ghost, send, recv, base, start, count):
     made = []
     for k in range(1, NC):
         copy = pltpu.make_async_remote_copy(
-            src_ref=mine,
-            dst_ref=ghost.at[place.c],
+            src_ref=mine.at[pl.ds(start, count)],
+            dst_ref=ghost.at[place.c, pl.ds(start, count)],
             send_sem=send.at[base + k - 1],
             recv_sem=recv.at[base + k - 1],
             device_id=place.member(k),
@@ -688,7 +688,7 @@
         )
         copy.start()
         made.append(copy)
-    ghost[place.c] = mine[...]
+    ghost[place.c, pl.ds(start, count), :] = mine[pl.ds(start, count), :]
     return made
 
 
@@ -759,8 +759,10 @@
     gather.relay()
     early.hand_on(tables, strips)
     late.send_own()
-    early.take(tables, strips, put_into(mine, QX))
-    shared = share(place, mine, landed, send, recv, base)
+    early.take(tables, strips, put_into(mine, QX), "A")
+    shared = share(place, mine, landed, send, recv, base, 0, QX)
+    early.take(tables, strips, put_into(mine, QX), "B")
+    shared += share(place, mine, landed, send, recv, base + 17, QX, QX)
     gather.take()
     span = CX * CY // NC
     for c in range(NC):
@@ -793,8 +795,10 @@
     each_x(middle, M0, M1)
     again.hand_on(tables, quarters)
     each_x(middle, M1, M2)
-    again.take(tables, quarters, put_into(mine1, QA))
-    shared1 = share(place, mine1, landed1, send, recv, base + 3)
+    again.take(tables, quarters, put_into(mine1, QA), "A")
+    shared1 = share(place, mine1, landed1, send, recv, base + 3, 0, QA)
+    again.take(tables, quarters, put_into(mine1, QA), "B")
+    shared1 += share(place, mine1, landed1, send, recv, base + 20, QA, QB)
     late.hand_on(tables, wholes)
     each_x(middle, M2, CX)
     late.take(tables, wholes, put_halves(wa, wb))
@@ -849,7 +853,7 @@
     whole = exchange_scratch(BIG, BIG, FACE, FACE)
     grid = [VMEM((NV * EXT, CZ), F32), VMEM((2 * FACE, CZ), F32), VMEM((2 * CY, CZ), F32)]
     half = VMEM((HALF, CZ), F32)
-    copies = 17 + 12 * N_COPIES
+    copies = 23 + 12 * N_COPIES
     adjoint, final = pl.pallas_call(
         kernel,
         out_shape=(block, block),

time: 76.1 us -> 76.3 us (level)
  no operation moved by 1% of the time
where the time goes in v8:
time: 76.3 us; the launch traced here: 76.2 us
  Pallas kernels  72.5 us (95%)
  local copies, waits for them, and re-layouts  3.05 us (4%)
    pallas_call x1, Pallas kernels, on_device(): pl.pallas_call(kernel, out_shape=(block, block), in_specs=[pl.BlockSpec(m...  72.5 us
    unnamed x4, local copies, waits for them, and re-layouts  3.05 us

profile of v8, /device:TPU:0, one launch (start us, length us, event | category | flops | bytes accessed | tf_op | source)
XLA Modules:
  0.0 76.2 jit_solution(858077768446774568)
XLA Ops:
  0.6 72.5 %shard_map.86 = (f32[1536,128]{1,0:T(8,128)}, f32[1536,128]{1,0:T(8,128)}) custom-call(s32[32]{0:T(128)} %owner.1, s32[6,32]{1,0:T(8,128)} %bitcast.12, s32[6,32]{1,0:T(8,128)} %bitcast.13, f32[3,6,6]{2,1,0:T(8,128)} %mats.1, f32[384,128]{1,0:T(8,128)} %bitcast.10, f32[1536,128]{1,0:T(8,128)} %bitcast.9, f32[256,128]{1,0:T(8,128)} %bitcast.11), custom_call_target="tpu_custom_call" | custom-call | tf_op jit(solution)/shard_map/pallas_call | solution.py:857
  73.1 0.0 copy-start
  73.1 2.2 %copy.11 = f32[1,1,6,16,16,128]{5,4,3,2,1,0:T(8,128)} copy(f32[1,1,6,16,16,128]{5,4,3,2,1,0:T(8,128)} %bitcast.8) | data formatting | bytes 1572864
  75.3 0.0 copy-done
  75.3 0.9 %copy.12 = f32[1,6,16,16,128]{4,3,2,1,0:T(8,128)} copy(f32[1,6,16,16,128]{4,3,2,1,0:T(8,128)S(1)} %bitcast.7) | data formatting | bytes 1572864
Async XLA Ops:
  73.1 2.2 %copy-start = (f32[1536,128]{1,0:T(8,128)S(1)}, f32[1536,128]{1,0:T(8,128)}, u32[]{:S(2)}) copy-start(f32[1536,128]{1,0:T(8,128)} %get-tuple-element.5) | copy-start | bytes 2359300
